TPU v7x, 32 devices: a whole 2x2x4 slice. The times are simulated.
32 devices in a mesh: samp: 4 (over y, x), box: 8 (over z, core).
Axes of the slice: x: 2, y: 2, z: 4, core: 2. Of those that a mesh axis runs over, the one named last changes fastest.
Arguments:
- pattern_a: float32 [1024, 2, 18432], P('box', None, 'samp'), may hold values from -6 to 6
- children_b: int32 [256, 8], P('box'), may hold values from -1 to 1023, as said below
- children_c: int32 [64, 8], P('box'), may hold values from -1 to 255, as said below
- theta_ab: float32 [96, 128], replicated, may hold values from -0.625 to 0.625
- theta_bc: float32 [128, 160], replicated, may hold values from -0.5 to 0.5
- phi_start_b: int32 [256], P('samp'), may hold values from 0 to 191, as said below
- phi_weight_b: float32 [4, 256], P(None, 'samp'), may hold values from -0.25 to 1
- phi_start_c: int32 [320], P('samp'), may hold values from 0 to 255, as said below
- phi_weight_c: float32 [4, 320], P(None, 'samp'), may hold values from -0.25 to 1
- translation: float32 [316, 2, 51200], P(None, None, 'samp'), may hold values from -0.1875 to 0.1875
- list_src: int32 [64, 32], P('box'), may hold values from 0 to 63
- list_vec: int32 [64, 32], P('box'), may hold values from 0 to 315
Outputs:
- incoming: float32 [64, 2, 51200], P('box', None, 'samp')
Inputs may be any that keep to these rules, and one draw needn't show every extreme that they name: `children_b`: entry o of a row is -1 or the level-A box in octant o = 4 ox + 2 oy + oz of that level-B box; level-B box p and its children lie on the same index of box, boxes p // 32 and c // 128 being equal; every level-A box is the child of exactly one level-B box. `children_c`: entry o of a row is -1 or the level-B box in octant o of that level-C box; p // 8 equals c // 32; every level-B box is the child of exactly one level-C box. phi_start_b[m] is (m * 192 // 256 - 1) or (m * 192 // 256 - 2), modulo 192. phi_start_c[m] is (m * 256 // 320 - 1) or (m * 256 // 320 - 2), modulo 256.
All inputs are finite; a program needn't handle non-finite values.
Results may differ from a plain program's by a relative error of at most 0.000071.
Values sent between devices are 32-bit elements; how exact they have to be, the bound alone decides.
A program may use at most 192 MiB of HBM per device.

v0:
```python
import functools
import math

import jax
import jax.numpy as jnp
import numpy as np
from jax import lax
from jax.experimental import pallas as pl
from jax.experimental.pallas import tpu as pltpu
from jax.sharding import PartitionSpec as P

SIZE_B = 8
SIZE_C = 16
LANES = 128
GROUP = 4


def window(first, last, n_child, n_parent):
    low = 0
    while (low - 1) * n_child // n_parent + 2 >= first:
        low -= 1
    high = 0
    while (high + 1) * n_child // n_parent - 2 <= last:
        high += 1
    return low, high + 1


def phase_table(parts, per_part, low, high, n_theta, size):
    n_phi = parts * per_part
    theta = np.pi * (np.arange(n_theta) + 0.5) / n_theta
    first = np.arange(parts)[:, None] * per_part
    phi = 2.0 * np.pi * (first + np.arange(low, high)[None]) / n_phi
    u_x = np.cos(phi)[..., None] * np.sin(theta)
    u_y = np.sin(phi)[..., None] * np.sin(theta)
    u_z = np.broadcast_to(np.cos(theta), u_x.shape)
    psi = []
    for o in range(8):
        s_x, s_y, s_z = 2 * (o >> 2 & 1) - 1, 2 * (o >> 1 & 1) - 1, 2 * (o & 1) - 1
        psi.append(0.5 * np.pi * size * (s_x * u_x + s_y * u_y + s_z * u_z))
    psi = np.stack(psi, axis=2)
    return np.concatenate([np.cos(psi), np.sin(psi)], axis=2).astype(np.float32)


def split(x):
    high = x.astype(jnp.bfloat16)
    return high, (x - high.astype(jnp.float32)).astype(jnp.bfloat16)


def split_outside(x):
    high = lax.reduce_precision(x, exponent_bits=8, mantissa_bits=7)
    return high.astype(jnp.bfloat16), (x - high).astype(jnp.bfloat16)


def mm(a, b):
    return jnp.dot(a, b, preferred_element_type=jnp.float32)


def aggregate_kernel(
    steps, az_step, wb, wc, out_rows,
    samp, idx_b, wgt_b, idx_c, wgt_c,
    x_ref, tab_ref, sb_ref, phb_ref, tbc_ref, sc_ref, phc_ref,
    o_ref, grid_a, grid_b,
):
    step = pl.program_id(0)
    count_a = x_ref.shape[0]
    rows_x = x_ref.shape[1]
    rows = x_ref.reshape(count_a * rows_x, LANES)
    for c in range(2):
        for q in range(az_step // GROUP):
            tiles = [
                split(rows[pl.ds(6 * q + 2 * j + c, count_a, stride=rows_x), :]) for j in range(3)
            ]
            for pair in range(2):
                high = jnp.concatenate([tiles[pair][0], tiles[pair + 1][0]], axis=1)
                low = jnp.concatenate([tiles[pair][1], tiles[pair + 1][1]], axis=1)
                both = mm(high, tab_ref[pair, 0]) + mm(low, tab_ref[pair, 0]) + mm(high, tab_ref[pair, 1])
                for k in range(2):
                    place = step * az_step + q * GROUP + pair * 2 + k
                    grid_a[place, c * count_a : (c + 1) * count_a, :] = both[:, k * LANES : (k + 1) * LANES]

    @pl.when(step == steps - 1)
    def _():
        count_b = sb_ref.shape[0] // 8
        n_theta_c = tbc_ref.shape[2]

        def level_b(m, carry):
            parts = []
            for c in range(2):
                here = slice(c * count_a, (c + 1) * count_a)
                value = wgt_b[0, m] * grid_a[idx_b[0, m], here, :]
                for k in range(1, 4):
                    value = value + wgt_b[k, m] * grid_a[idx_b[k, m], here, :]
                parts.append(split(value))
            stacked = jnp.concatenate(
                [
                    jnp.concatenate([parts[0][0], parts[1][0]], axis=1),
                    jnp.concatenate([parts[0][1], parts[1][1]], axis=1),
                ],
                axis=0,
            )
            picked = mm(sb_ref[...], stacked)
            real = jnp.zeros((count_b, LANES), jnp.float32)
            imag = jnp.zeros((count_b, LANES), jnp.float32)
            for o in range(8):
                cosine = phb_ref[m, o : o + 1, :]
                sine = phb_ref[m, 8 + o : 9 + o, :]
                pr = picked[o * count_b : (o + 1) * count_b, :LANES]
                pi = picked[o * count_b : (o + 1) * count_b, LANES:]
                real = real + pr * cosine - pi * sine
                imag = imag + pr * sine + pi * cosine
            high, low = split(jnp.concatenate([real, imag], axis=0))
            both = jnp.concatenate([high, low], axis=1)
            grid_b[m] = mm(both, tbc_ref[0]) + mm(high, tbc_ref[1, :LANES])
            return carry

        lax.fori_loop(0, wb, level_b, 0)

        count_c = sc_ref.shape[0] // 8

        def level_c(g, carry):
            reals, imags = [], []
            for i in range(GROUP):
                n = g * GROUP + i
                value = wgt_c[0, n] * grid_b[idx_c[0, n]]
                for k in range(1, 4):
                    value = value + wgt_c[k, n] * grid_b[idx_c[k, n]]
                high, low = split(value)
                rr = mm(sc_ref[...], jnp.concatenate([high[:count_b], low[:count_b]], axis=0))
                ri = mm(sc_ref[...], jnp.concatenate([high[count_b:], low[count_b:]], axis=0))
                real = jnp.zeros((count_c, n_theta_c), jnp.float32)
                imag = jnp.zeros((count_c, n_theta_c), jnp.float32)
                for o in range(8):
                    cosine = phc_ref[n, o : o + 1, :]
                    sine = phc_ref[n, 8 + o : 9 + o, :]
                    pr = rr[o * count_c : (o + 1) * count_c]
                    pi = ri[o * count_c : (o + 1) * count_c]
                    real = real + pr * cosine - pi * sine
                    imag = imag + pr * sine + pi * cosine
                reals.append(real)
                imags.append(imag)
            for c, flat in enumerate((jnp.concatenate(reals, axis=1), jnp.concatenate(imags, axis=1))):
                tiles = flat.shape[1] // LANES
                for t in range(tiles):
                    o_ref[pl.ds(g * 2 * tiles + 2 * t + c, count_c, stride=out_rows), :] = flat[
                        :, t * LANES : (t + 1) * LANES
                    ]
            return carry

        lax.fori_loop(0, wc // GROUP, level_c, 0)


def translate_kernel(list_len, chunk, src, vec, x_ref, t_hbm, o_ref, real, imag, buf, sem):
    p = pl.program_id(0)
    count = pl.num_programs(0)
    n_src, samples = x_ref.shape[0], x_ref.shape[2]
    slot = lax.rem(p, 2)

    def fetch(target, where):
        def one(l, carry):
            pltpu.make_async_copy(
                t_hbm.at[vec[target * list_len + l]], buf.at[where, l], sem.at[where]
            ).start()
            return carry

        lax.fori_loop(0, list_len, one, 0)

    @pl.when(p == 0)
    def _():
        fetch(0, 0)

    @pl.when(p + 1 < count)
    def _():
        fetch(p + 1, 1 - slot)

    @pl.when(p == 0)
    def _():
        def one(s, carry):
            for r in range(0, samples, chunk):
                here = slice(r, r + chunk)
                real[s, :, here] = jnp.broadcast_to(x_ref[s, 0:1, here], (2, chunk))
                imag[s, :, here] = jnp.broadcast_to(x_ref[s, 1:2, here], (2, chunk))
            return carry

        lax.fori_loop(0, n_src, one, 0)

    def drain(l, carry):
        pltpu.make_async_copy(t_hbm.at[0], buf.at[slot, l], sem.at[slot]).wait()
        return carry

    lax.fori_loop(0, list_len, drain, 0)

    def one_chunk(i, carry):
        r = pl.ds(pl.multiple_of(i * chunk, chunk), chunk)
        by_real = jnp.zeros((2, chunk), jnp.float32)
        by_imag = jnp.zeros((2, chunk), jnp.float32)
        for l in range(list_len):
            s = src[p * list_len + l]
            t = buf[slot, l, :, r]
            by_real = by_real + t * real[s, :, r]
            by_imag = by_imag + t * imag[s, :, r]
        o_ref[0, 0:1, r] = by_real[0:1] - by_imag[1:2]
        o_ref[0, 1:2, r] = by_imag[0:1] + by_real[1:2]
        return carry

    lax.fori_loop(0, samples // chunk, one_chunk, 0)


def pick_chunk(samples):
    for tiles in (20, 16, 12, 8, 4, 2, 1):
        if samples % (tiles * LANES) == 0:
            return tiles * LANES
    return samples


def interleave(x):
    return x.reshape(x.shape[0], 2, -1, LANES).transpose(0, 2, 1, 3).reshape(x.shape[0], -1, LANES)


def stencil(start, weight, first, low, high, src_low, src_high, n_child):
    nearest = start - first
    tap = nearest[None, :] + jnp.arange(4, dtype=jnp.int32)[:, None]
    half = n_child // 2
    tap = (tap + half) % n_child - half
    centre = (src_low + src_high) // 2
    tap = jnp.where(tap - centre > half, tap - n_child, tap)
    tap = jnp.where(tap - centre < -half, tap + n_child, tap)
    inside = (tap >= src_low) & (tap < src_high)
    rows = jnp.clip(tap - src_low, 0, src_high - src_low - 1)
    return rows.astype(jnp.int32), jnp.where(inside, weight, 0.0)


def one_hot(children, first, count):
    ids = (children - first).T.reshape(-1)
    hot = ((ids[:, None] == jnp.arange(count)[None, :]) & (children.T.reshape(-1) >= 0)[:, None]).astype(jnp.bfloat16)
    return jnp.concatenate([hot, hot], axis=1)


def per_device(
    n_samp,
    pattern_a, children_b, children_c, theta_ab, theta_bc,
    phi_start_b, phi_weight_b, phi_start_c, phi_weight_c,
    translation, list_src, list_vec,
):
    samp = lax.axis_index("samp")
    box = lax.axis_index("box")
    count_a, count_b, count_c = pattern_a.shape[0], children_b.shape[0], children_c.shape[0]
    theta_a, theta_b = theta_ab.shape
    theta_c = theta_bc.shape[1]
    pa = pattern_a.shape[2] // theta_a
    pb = phi_start_b.shape[0]
    pc = phi_start_c.shape[0]
    n_a, n_b, n_c = n_samp * pa, n_samp * pb, n_samp * pc
    low_b, high_b = window(0, pa - 1, n_a, n_b)
    low_c, high_c = window(low_b, high_b - 1, n_b, n_c)
    ext = -(-max(-low_c, high_c - pc) // GROUP) * GROUP
    low_c, high_c = -ext, pc + ext
    wb, wc = high_b - low_b, high_c - low_c

    up = [(i, (i + 1) % n_samp) for i in range(n_samp)]
    down = [((i + 1) % n_samp, i) for i in range(n_samp)]
    table_b = jnp.concatenate([phi_start_b.astype(jnp.float32)[None], phi_weight_b], axis=0)
    table_c = jnp.concatenate([phi_start_c.astype(jnp.float32)[None], phi_weight_c], axis=0)
    near = max(ext, -low_b, high_b - pb)
    left = lax.ppermute(jnp.concatenate([table_b[:, pb - near :], table_c[:, pc - near :]], 1), "samp", up)
    right = lax.ppermute(jnp.concatenate([table_b[:, :near], table_c[:, :near]], 1), "samp", down)
    table_b = jnp.concatenate([left[:, near + low_b : near], table_b, right[:, : high_b - pb]], 1)
    table_c = jnp.concatenate([left[:, 2 * near - ext :], table_c, right[:, near : near + ext]], 1)
    idx_b, wgt_b = stencil(
        table_b[0].astype(jnp.int32), table_b[1:], samp * pa, low_b, high_b, 0, pa, n_a
    )
    idx_c, wgt_c = stencil(
        table_c[0].astype(jnp.int32), table_c[1:], samp * pb, low_c, high_c, low_b, high_b, n_b
    )

    tab = []
    for pair in range(2):
        at = pair * (2 * theta_a - LANES)
        blocks = jnp.zeros((2 * LANES, 2 * theta_b), jnp.float32)
        for k in range(2):
            blocks = lax.dynamic_update_slice(blocks, theta_ab, (at + k * theta_a, k * theta_b))
        tab.append(jnp.stack(split_outside(blocks)))
    tab = jnp.stack(tab)
    high, low = split_outside(theta_bc)
    tbc = jnp.stack([jnp.concatenate([high, high], 0), jnp.concatenate([low, low], 0)])
    s_b = one_hot(children_b, box * count_a, count_a)
    s_c = one_hot(children_c, box * count_b, count_b)
    phb = jnp.asarray(phase_table(n_samp, pb, low_b, high_b, theta_b, SIZE_B))
    phc = jnp.asarray(phase_table(n_samp, pc, low_c, high_c, theta_c, SIZE_C))

    x = interleave(pattern_a)
    steps = pa // 16 if pa % 16 == 0 else 1
    x = jnp.pad(x, ((0, 0), (0, -x.shape[1] % 8), (0, 0)))
    rows_x = x.shape[1]
    az_step = pa // steps
    tiles = GROUP * theta_c // LANES
    out_rows = wc // GROUP * 2 * tiles
    ext_rows = ext // GROUP * 2 * tiles
    rows = pc // GROUP * 2 * tiles
    one = pl.Buffered(1)
    wide = pl.pallas_call(
        functools.partial(aggregate_kernel, steps, az_step, wb, wc, out_rows),
        grid_spec=pltpu.PrefetchScalarGridSpec(
            num_scalar_prefetch=5,
            grid=(steps,),
            in_specs=[
                pl.BlockSpec((count_a, rows_x // steps, LANES), lambda i, *_: (0, i, 0)),
                pl.BlockSpec(tab.shape, lambda i, *_: (0, 0, 0, 0), pipeline_mode=one),
                pl.BlockSpec(s_b.shape, lambda i, *_: (0, 0), pipeline_mode=one),
                pl.BlockSpec((None,) + phb.shape[1:], lambda i, s, *_: (s[0], 0, 0, 0), pipeline_mode=one),
                pl.BlockSpec(tbc.shape, lambda i, *_: (0, 0, 0), pipeline_mode=one),
                pl.BlockSpec(s_c.shape, lambda i, *_: (0, 0), pipeline_mode=one),
                pl.BlockSpec((None,) + phc.shape[1:], lambda i, s, *_: (s[0], 0, 0, 0), pipeline_mode=one),
            ],
            out_specs=pl.BlockSpec((count_c * out_rows, LANES), lambda i, *_: (0, 0)),
            scratch_shapes=[
                pltpu.VMEM((pa, 2 * count_a, LANES), jnp.float32),
                pltpu.VMEM((wb, 2 * count_b, theta_c), jnp.float32),
            ],
        ),
        out_shape=jax.ShapeDtypeStruct((count_c * out_rows, LANES), jnp.float32),
        compiler_params=pltpu.CompilerParams(vmem_limit_bytes=48 << 20),
        name="aggregate",
    )(samp.reshape(1), idx_b, wgt_b, idx_c, wgt_c, x, tab, s_b, phb, tbc, s_c, phc)
    wide = wide.reshape(count_c, out_rows, LANES)
    from_left = lax.ppermute(wide[:, out_rows - ext_rows :], "samp", up)
    from_right = lax.ppermute(wide[:, :ext_rows], "samp", down)
    zeros = jnp.zeros((count_c, rows - ext_rows, LANES), jnp.float32)
    mine = (
        wide[:, ext_rows : out_rows - ext_rows]
        + jnp.concatenate([from_left, zeros], 1)
        + jnp.concatenate([zeros, from_right], 1)
    )
    mine = mine.reshape(count_c, rows // 2, 2, LANES).transpose(0, 2, 1, 3).reshape(count_c, 2, -1)
    everyone = lax.all_gather(mine, "box", axis=0, tiled=True)

    list_len = list_src.shape[1]
    n_src, _, samples = everyone.shape
    chunk = pick_chunk(samples)
    return pl.pallas_call(
        functools.partial(translate_kernel, list_len, chunk),
        grid_spec=pltpu.PrefetchScalarGridSpec(
            num_scalar_prefetch=2,
            grid=(count_c,),
            in_specs=[
                pl.BlockSpec(everyone.shape, lambda i, *_: (0, 0, 0), pipeline_mode=one),
                pl.BlockSpec(memory_space=pl.ANY),
            ],
            out_specs=pl.BlockSpec((1, 2, samples), lambda i, *_: (i, 0, 0)),
            scratch_shapes=[
                pltpu.VMEM(everyone.shape, jnp.float32),
                pltpu.VMEM(everyone.shape, jnp.float32),
                pltpu.VMEM((2, list_len, 2, samples), jnp.float32),
                pltpu.SemaphoreType.DMA((2,)),
            ],
        ),
        out_shape=jax.ShapeDtypeStruct((count_c, 2, samples), jnp.float32),
        compiler_params=pltpu.CompilerParams(vmem_limit_bytes=48 << 20),
        name="translate",
    )(list_src.reshape(-1), list_vec.reshape(-1), everyone, translation)


def solution(mesh):
    placed = (
        P("box", None, "samp"),
        P("box", None),
        P("box", None),
        P(),
        P(),
        P("samp"),
        P(None, "samp"),
        P("samp"),
        P(None, "samp"),
        P(None, None, "samp"),
        P("box", None),
        P("box", None),
    )
    return jax.shard_map(
        functools.partial(per_device, mesh.shape["samp"]),
        mesh=mesh, in_specs=placed, out_specs=P("box", None, "samp"), check_vma=False,
    )
```

profile of v0, /device:TPU:0, one launch (start us, length us, event | category | flops | bytes accessed | tf_op | source)
XLA Modules:
  0.0 181.3 jit_solution(2948791527177083091)
XLA Ops:
  6.5 0.7 convert_bitcast_fusion.1
  7.2 0.7 convert_bitcast_fusion
  7.9 0.7 pad_maximum_fusion.2
  8.5 0.7 pad_maximum_fusion.3
  9.2 0.1 fusion.16
  9.3 0.1 pad_maximum_fusion.5
  9.4 3.9 %collective-permute-start.1 = (f32[5,16]{1,0:T(8,128)S(1)}, f32[5,16]{1,0:T(8,128)S(1)}, u32[]{:S(2)}, u32[]{:S(2)}) collective-permute-start(f32[5,16]{1,0:T(8,128)S(1)} %pad_maximum_fusion.5), channel_id=1, source_target_pairs={{8,0},{16,8},{24,16},{0,24},{9,1},{17,9},{25,17},{1,25},{10,2},{18... | collective-permute-start | bytes 968 | tf_op jit(solution)/shard_map/ppermute | solution.py:265
  13.3 0.1 pad_maximum_fusion.4
  13.4 0.9 reduce_precision.11
  14.3 1.0 copy.45
  15.3 0.9 fusion.15
  16.2 0.7 compare_bitcast_fusion.1
  16.9 0.7 subtract_bitcast_fusion.1
  17.6 0.1 eq.34
  17.6 0.1 ge.44
  17.7 0.1 fusion.7
  17.9 0.1 copy.44
  18.0 0.7 compare_bitcast_fusion
  18.7 0.7 subtract_bitcast_fusion
  19.4 0.1 copy.47
  19.5 0.1 eq.38
  19.5 0.1 copy.48
  19.6 0.1 ge.48
  19.7 0.1 fusion.8
  19.8 0.1 add_convert_fusion.1.sc_ref
  19.9 0.8 constant_dynamic-update-slice_fusion.1
  20.7 0.1 fusion.5
  20.9 0.1 pad_maximum_fusion.tab_ref
  21.0 8.1 %copy.42 = f32[128,2,4608]{0,2,1:T(8,128)} copy(f32[128,2,4608]{2,1,0:T(2,128)} %param.14) | data formatting | bytes 9437184 | tf_op args[0]
  29.1 8.3 %copy.43 = f32[128,36,2,128]{3,2,1,0:T(2,128)} copy(f32[128,36,2,128]{0,3,1,2:T(8,128)} %bitcast.45) | data formatting | bytes 9437184 | tf_op jit(solution)/shard_map/transpose | solution.py:216
  37.5 0.1 slice.47
  37.5 0.1 pad_maximum_fusion.6
  37.7 0.1 slice.54
  37.8 0.1 slice.53
  37.8 0.1 pad_maximum_fusion.7
  38.0 41.4 %aggregate.1 = f32[1920,128]{1,0:T(8,128)S(1)} custom-call(s32[1]{0:T(128)} %bitcast.samp, s32[4,69]{1,0:T(4,128)S(1)} %broadcast_clamp_fusion.idx_b, f32[4,69]{1,0:T(4,128)S(1)} %slice_select_fusion.1.wgt_b, s32[4,96]{1,0:T(4,128)S(1)} %add_clamp_fusion.idx_c, f32[4,96]{1,0:T(4,128)S(1)} %slice_select_fusion.wgt_c, f32[128,72,128]{2,1,0:T(8,128)} %bitcast.44, ...), custom_call_target="tpu_custom_call" | custom-call | tf_op jit(solution)/shard_map/aggregate/pallas_call | solution.py:300
  79.5 3.0 %collective-permute-start.3 = (f32[8,20,128]{2,0,1:T(8,128)S(1)}, f32[8,20,128]{2,0,1:T(8,128)S(1)}, u32[]{:S(2)}, u32[]{:S(2)}) collective-permute-start(f32[8,20,128]{2,0,1:T(8,128)S(1)} %copy.58), channel_id=1, source_target_pairs={{8,0},{16,8},{24,16},{0,24},{9,1},{17,9},{25,17},{1,25},{10,2},{18... | collective-permute-start | bytes 245768 | tf_op jit(solution)/shard_map/ppermute | solution.py:326
  82.5 0.1 collective-permute-start.2
  82.5 0.1 slice.60
  82.6 1.9 %collective-permute-done.3 = f32[8,20,128]{2,0,1:T(8,128)S(1)} collective-permute-done((f32[8,20,128]{2,0,1:T(8,128)S(1)}, f32[8,20,128]{2,0,1:T(8,128)S(1)}, u32[]{:S(2)}, u32[]{:S(2)}) %collective-permute-start.3) | collective-permute-done | bytes 81952 | tf_op jit(solution)/shard_map/ppermute | solution.py:326
  84.5 3.4 %collective-permute-done.2 = f32[8,20,128]{2,0,1:T(8,128)S(1)} collective-permute-done((f32[8,20,128]{2,0,1:T(8,128)S(1)}, f32[8,20,128]{2,0,1:T(8,128)S(1)}, u32[]{:S(2)}, u32[]{:S(2)}) %collective-permute-start.2) | collective-permute-done | bytes 81952 | tf_op jit(solution)/shard_map/ppermute | solution.py:325
  87.9 0.2 fusion
  88.0 0.3 copy.54
  88.3 1.4 reshape.50
  89.7 0.1 reshape.42.src
  89.8 0.1 reshape.43.vec
  89.9 66.2 %all-gather.2.cloned.1.call-done.x_ref = f32[64,2,12800]{2,1,0:T(2,128)} async-done(((f32[8,2,12800]{2,1,0:T(2,128)}), f32[64,2,12800]{2,1,0:T(2,128)}) %all-gather.2.cloned.1.call-update) | async-done | bytes 6553616 | tf_op jit(solution)/shard_map/all_gather | solution.py:334
  156.1 18.4 %translate.1 = f32[8,2,12800]{2,1,0:T(2,128)} custom-call(s32[256]{0:T(256)S(1)} %reshape.42.src, s32[256]{0:T(256)S(1)} %reshape.43.vec, f32[64,2,12800]{2,1,0:T(2,128)} %all-gather.2.cloned.1.call-done.x_ref, f32[316,2,12800]{2,1,0:T(2,128)} %t_hbm.1), custom_call_target="tpu_custom_call" | custom-call | tf_op jit(solution)/shard_map/translate/pallas_call | solution.py:339
  (30 shorter events, 0.4 us)
Async XLA Ops:
  6.5 149.5 %all-gather.2.cloned.1.call-start = ((), (), s32[]{:S(2)}) async-start(), calls=%async_computation | async-start | bytes 7372800 | tf_op jit(solution)/shard_map/all_gather | solution.py:334
  9.4 28.2 %collective-permute-start.1 = (f32[5,16]{1,0:T(8,128)S(1)}, f32[5,16]{1,0:T(8,128)S(1)}, u32[]{:S(2)}, u32[]{:S(2)}) collective-permute-start(f32[5,16]{1,0:T(8,128)S(1)} %pad_maximum_fusion.5), channel_id=1, source_target_pairs={{8,0},{16,8},{24,16},{0,24},{9,1},{17,9},{25,17},{1,25},{10,2},{18... | collective-permute-start | bytes 968 | tf_op jit(solution)/shard_map/ppermute | solution.py:265
  13.4 24.1 %collective-permute-start = (f32[5,16]{1,0:T(8,128)S(1)}, f32[5,16]{1,0:T(8,128)S(1)}, u32[]{:S(2)}, u32[]{:S(2)}) collective-permute-start(f32[5,16]{1,0:T(8,128)S(1)} %pad_maximum_fusion.4), channel_id=1, source_target_pairs={{0,8},{8,16},{16,24},{24,0},{1,9},{9,17},{17,25},{25,1},{2,10},{10... | collective-permute-start | bytes 968 | tf_op jit(solution)/shard_map/ppermute | solution.py:264
  29.1 8.4 %copy-start.1 = (f32[4,64]{1,0:T(4,128)S(1)}, f32[4,64]{1,0:T(4,128)}, u32[]{:S(2)}) copy-start(f32[4,64]{1,0:T(4,128)} %param.20) | copy-start | bytes 3076
  29.1 8.7 %copy-start.2 = (f32[4,80]{1,0:T(4,128)S(1)}, f32[4,80]{1,0:T(4,128)}, u32[]{:S(2)}) copy-start(f32[4,80]{1,0:T(4,128)} %param.22) | copy-start | bytes 3844
  29.1 8.8 %copy-start = (f32[4,69,16,128]{3,2,1,0:T(8,128)S(1)}, f32[4,69,16,128]{3,2,1,0:T(8,128)}, u32[]{:S(2)}) copy-start(f32[4,69,16,128]{3,2,1,0:T(8,128)} %constant.97.clone.phb_ref) | copy-start | bytes 6782980
  79.4 10.3 %copy-start.3 = (s32[8,32]{1,0:T(8,128)S(1)}, s32[8,32]{1,0:T(8,128)}, u32[]{:S(2)}) copy-start(s32[8,32]{1,0:T(8,128)} %param.24) | copy-start | bytes 3076
  79.4 10.4 %copy-start.4 = (s32[8,32]{1,0:T(8,128)S(1)}, s32[8,32]{1,0:T(8,128)}, u32[]{:S(2)}) copy-start(s32[8,32]{1,0:T(8,128)} %param.25) | copy-start | bytes 3076
  79.5 5.0 %collective-permute-start.3 = (f32[8,20,128]{2,0,1:T(8,128)S(1)}, f32[8,20,128]{2,0,1:T(8,128)S(1)}, u32[]{:S(2)}, u32[]{:S(2)}) collective-permute-start(f32[8,20,128]{2,0,1:T(8,128)S(1)} %copy.58), channel_id=1, source_target_pairs={{8,0},{16,8},{24,16},{0,24},{9,1},{17,9},{25,17},{1,25},{10,2},{18... | collective-permute-start | bytes 245768 | tf_op jit(solution)/shard_map/ppermute | solution.py:326
  82.5 5.4 %collective-permute-start.2 = (f32[8,20,128]{2,0,1:T(8,128)S(1)}, f32[8,20,128]{2,0,1:T(8,128)S(1)}, u32[]{:S(2)}, u32[]{:S(2)}) collective-permute-start(f32[8,20,128]{2,0,1:T(8,128)S(1)} %copy.57), channel_id=1, source_target_pairs={{0,8},{8,16},{16,24},{24,0},{1,9},{9,17},{17,25},{25,1},{2,10},{10... | collective-permute-start | bytes 245768 | tf_op jit(solution)/shard_map/ppermute | solution.py:325
Sparse Core Ops, SparseCore 0:
  89.8 66.2 all-gather.1
where the time goes:
time: 183 us; the launch traced here: 181 us
  waiting for transfers between devices  71.5 us (39%)
  Pallas kernels  59.8 us (33%)
  local copies, waits for them, and re-layouts  21.9 us (12%)
  between operations  13.6 us (7%)
  other arithmetic  7.52 us (4%)
  starting transfers between devices  6.96 us (4%)
    all_gather x1, waiting for transfers between devices, per_device(): everyone = lax.all_gather(mine, 'box', axis=0, tiled=True)  66.2 us
    pallas_call x1, Pallas kernels, per_device(): pl.pallas_call(functools.partial(aggregate_kernel, steps, az_step, wb, wc...  41.4 us
    pallas_call x1, Pallas kernels, per_device(): pl.pallas_call(functools.partial(translate_kernel, list_len, chunk), grid...  18.4 us
    unnamed x14, local copies, waits for them, and re-layouts  9.14 us
    transpose x1, local copies, waits for them, and re-layouts, interleave(): x.reshape(x.shape[0], 2, -1, LANES).transpose(0, 2, 1, 3)  8.32 us
    ppermute x1, starting transfers between devices, per_device(): lax.ppermute(jnp.concatenate([table_b[:, :near], table_c[:, :near]], 1),...  3.92 us
  transfers between devices with their start and end apart: 5, of which 3 were waited for; matrix products, arithmetic and copies ran while one was open for 13% of the time, Pallas kernels for 0%

commit v1 on v0

--- a/solution.py
+++ b/solution.py
@@ -6,12 +6,15 @@
 import numpy as np
 from jax import lax
 from jax.experimental import pallas as pl
+from jax.experimental.layout import Layout, with_layout_constraint
 from jax.experimental.pallas import tpu as pltpu
 from jax.sharding import PartitionSpec as P
 
 SIZE_B = 8
 SIZE_C = 16
 LANES = 128
+MESH = pl.DeviceIdType.MESH
+CHUNK = 2
 GROUP = 4
 
 
@@ -56,7 +59,7 @@
 
 
 def aggregate_kernel(
-    steps, az_step, wb, wc, out_rows,
+    steps, az_step, wb, wc, ext, plan,
     samp, idx_b, wgt_b, idx_c, wgt_c,
     x_ref, tab_ref, sb_ref, phb_ref, tbc_ref, sc_ref, phc_ref,
     o_ref, grid_a, grid_b,
@@ -116,6 +119,8 @@
         lax.fori_loop(0, wb, level_b, 0)
 
         count_c = sc_ref.shape[0] // 8
+        o_ref[...] = jnp.zeros(o_ref.shape, jnp.float32)
+        edge, inner = ext // GROUP, wc // GROUP - 2 * (ext // GROUP)
 
         def level_c(g, carry):
             reals, imags = [], []
@@ -140,8 +145,17 @@
                 imags.append(imag)
             for c, flat in enumerate((jnp.concatenate(reals, axis=1), jnp.concatenate(imags, axis=1))):
                 tiles = flat.shape[1] // LANES
+                base = jnp.where(
+                    g < edge,
+                    plan.padded + plan.left_pad + g * 2 * tiles,
+                    jnp.where(
+                        g < edge + inner,
+                        (g - edge) * 2 * tiles,
+                        plan.padded + plan.left_rows + (g - edge - inner) * 2 * tiles,
+                    ),
+                )
                 for t in range(tiles):
-                    o_ref[pl.ds(g * 2 * tiles + 2 * t + c, count_c, stride=out_rows), :] = flat[
+                    o_ref[pl.ds(base + 2 * t + c, count_c, stride=plan.total), :] = flat[
                         :, t * LANES : (t + 1) * LANES
                     ]
             return carry
@@ -149,71 +163,325 @@
         lax.fori_loop(0, wc // GROUP, level_c, 0)
 
 
-def translate_kernel(list_len, chunk, src, vec, x_ref, t_hbm, o_ref, real, imag, buf, sem):
-    p = pl.program_id(0)
-    count = pl.num_programs(0)
-    n_src, samples = x_ref.shape[0], x_ref.shape[2]
-    slot = lax.rem(p, 2)
-
-    def fetch(target, where):
-        def one(l, carry):
+def far_kernel(
+    plan, list_len, n_samp, wide, lists, t_hbm, o_ref,
+    list_all, list_smem, halo_left, halo_right, swapped, res, psend, precv, *rest,
+):
+    n_chunk = len(plan.sizes)
+    srcs, tbufs = rest[:n_chunk], rest[n_chunk : 2 * n_chunk]
+    (list_sem, smem_sem, halo_sem, t_sem, src_send, src_recv, p_sem, out_sem) = rest[2 * n_chunk :]
+    samp, box = lax.axis_index("samp"), lax.axis_index("box")
+    n_box = plan.n_box
+    n_chip = n_box // 2
+    chip, core = box // 2, box % 2
+    partner = chip * 2 + 1 - core
+    own = wide.shape[0]
+    first_end, last_end = chip == 0, chip == n_chip - 1
+    is_end = first_end | last_end
+    helps_first, helps_last = chip == 1, chip == n_chip - 2
+    helps = helps_first | helps_last
+    helped = jnp.where(helps_first, 0, n_chip - 1)
+    helper = jnp.where(first_end, 1, n_chip - 2)
+    left = (lax.rem(samp + n_samp - 1, n_samp), box)
+    right = (lax.rem(samp + 1, n_samp), box)
+
+    def remote(src, dst, send, recv, device):
+        return pltpu.make_async_remote_copy(
+            src_ref=src, dst_ref=dst, send_sem=send, recv_sem=recv, device_id=device, device_id_type=MESH
+        )
+
+    barrier = pltpu.get_barrier_semaphore()
+    for other in range(n_box):
+        @pl.when(box != other)
+        def _():
+            pl.semaphore_signal(barrier, inc=1, device_id=(samp, other), device_id_type=MESH)
+    for device in (left, right):
+        pl.semaphore_signal(barrier, inc=1, device_id=device, device_id_type=MESH)
+    pl.semaphore_wait(barrier, n_box + 1)
+
+    def half_rows(which, c):
+        count = 8 * plan.sizes[c]
+        low = 8 * (plan.split - plan.starts[c]) - count
+        high = 8 * (plan.split + plan.starts[c])
+        return pl.ds(pl.multiple_of(jnp.where(which == 0, low, high), 8), count)
+
+    def has(which, c):
+        return (which == 0) | plan.both[c]
+
+    def t_copy(c):
+        return pltpu.make_async_copy(t_hbm.at[:, half_rows(core, c), :], tbufs[c], t_sem.at[c])
+
+    def when_has(which, c, do):
+        if plan.both[c]:
+            do()
+        else:
+            pl.when(which == 0)(do)
+
+    to_left = remote(wide.at[:, plan.left_at, :], halo_right, halo_sem.at[0], halo_sem.at[1], left)
+    to_right = remote(wide.at[:, plan.right_at, :], halo_left, halo_sem.at[2], halo_sem.at[3], right)
+    to_left.start()
+    to_right.start()
+
+    def list_copy(slot, device, k):
+        return remote(lists, list_all.at[slot], list_sem.at[k], list_sem.at[3 + slot], device)
+
+    list_copy(core, (samp, partner), 0).start()
+
+    @pl.when(is_end)
+    def _():
+        for d in range(2):
+            list_copy(2 + core, (samp, helper * 2 + d), 1 + d).start()
+
+    def src_copy(c, chip_to, d):
+        index = c * n_box + chip_to * 2 + d
+        return remote(
+            wide.at[:, half_rows(d, c), :],
+            srcs[c].at[pl.ds(pl.multiple_of(own * box, 8), own)],
+            src_send.at[index],
+            src_recv.at[c * n_box + box],
+            (samp, chip_to * 2 + d),
+        )
+
+    def send_chunk(c, act):
+        def to_partner():
+            act(src_copy(c, chip, 1 - core))
+
+        when_has(1 - core, c, to_partner)
+        for chip_to in range(1, n_chip - 1):
+            @pl.when(chip != chip_to)
+            def _():
+                for d in range(2):
+                    if d == 0 or plan.both[c]:
+                        act(src_copy(c, chip_to, d))
+
+    for c in range(plan.early):
+        send_chunk(c, lambda copy: copy.start())
+    for c in range(n_chunk):
+        when_has(core, c, lambda c=c: t_copy(c).start())
+
+    list_all[core] = lists[...]
+    to_left.wait_recv()
+    to_right.wait_recv()
+    at_end = pl.ds(plan.end_at, halo_right.shape[1])
+    wide[:, at_end, :] = wide[:, at_end, :] + halo_right[...]
+    at_start = pl.ds(0, halo_left.shape[1])
+    wide[:, at_start, :] = wide[:, at_start, :] + halo_left[...]
+    for c in range(plan.early, n_chunk):
+        send_chunk(c, lambda copy: copy.start())
+
+    list_copy(1 - core, (samp, partner), 0).wait_recv()
+
+    @pl.when(helps)
+    def _():
+        for d in range(2):
+            list_copy(2 + d, (samp, partner), 0).wait_recv()
+
+    n_src = own * n_box
+    low = jnp.where(last_end, n_src - 2 * own, 0)
+    high = jnp.where(first_end, 2 * own, n_src)
+    low_p = jnp.where(helps_first, 2 * own, 0)
+    high_p = jnp.where(helps_last, n_src - 2 * own, n_src)
+    lane = lax.broadcasted_iota(jnp.int32, list_all.shape[1:], 1)
+    for slot in range(4):
+        a, b = (low, high) if slot < 2 else (low_p, high_p)
+        value = list_all[slot]
+        gone = (lane < list_len) & ((value < a) | (value >= b))
+        list_all[slot] = jnp.where(gone, n_src, value)
+    to_smem = pltpu.make_async_copy(list_all, list_smem, smem_sem)
+    to_smem.start()
+    to_smem.wait()
+
+    even = lax.rem(lax.broadcasted_iota(jnp.int32, (8, LANES), 0), 2) == 0
+
+    def turn(x):
+        return jnp.where(even, pltpu.roll(x, 7, 0), pltpu.roll(x, 1, 0))
+
+    def gather_sum(c, slot, i):
+        size = plan.sizes[c]
+        by_same = [jnp.zeros((8, LANES), jnp.float32) for _ in range(size)]
+        by_turned = [jnp.zeros((8, LANES), jnp.float32) for _ in range(size)]
+        for l in range(list_len):
+            s = list_smem[slot, i, l]
+            v = list_smem[slot, i, list_len + l]
+            for g in range(size):
+                here = slice(8 * g, 8 * g + 8)
+                t = tbufs[c][v, here, :]
+                by_same[g] = by_same[g] + t * srcs[c][s, here, :]
+                by_turned[g] = by_turned[g] + t * swapped[s, here, :]
+        out = []
+        for g in range(size):
+            x, y = by_same[g], by_turned[g]
+            out.append(jnp.where(even, x - pltpu.roll(x, 7, 0), y + pltpu.roll(y, 1, 0)))
+        return out
+
+    def result_copy(c):
+        return remote(
+            res.at[pl.ds(pl.multiple_of((1 - core) * own, 8), own), plan.local[c], :],
+            o_ref.at[:, half_rows(core, c), :],
+            out_sem.at[c],
+            out_sem.at[n_chunk + c],
+            (samp, partner),
+        )
+
+    def result_wait(c):
+        return remote(
+            res.at[pl.ds(pl.multiple_of((1 - core) * own, 8), own), plan.local[c], :],
+            o_ref.at[:, half_rows(1 - core, c), :],
+            out_sem.at[c],
+            out_sem.at[n_chunk + c],
+            (samp, partner),
+        )
+
+    def p_copy(c, chip_to):
+        return remote(
+            psend.at[:, plan.local[c], :],
+            precv.at[:, plan.local[c], :],
+            p_sem.at[c],
+            p_sem.at[n_chunk + c],
+            (samp, chip_to * 2 + core),
+        )
+
+    def one_chunk(c):
+        size = plan.sizes[c]
+        rows = 8 * size
+        place = plan.local[c]
+        srcs[c][pl.ds(pl.multiple_of(own * box, 8), own)] = wide[:, half_rows(core, c), :]
+        srcs[c][pl.ds(n_src, 8)] = jnp.zeros((8, rows, LANES), jnp.float32)
+        swapped[pl.ds(n_src, 8)] = jnp.zeros((8, swapped.shape[1], LANES), jnp.float32)
+        t_copy(c).wait()
+
+        def arrived(other):
             pltpu.make_async_copy(
-                t_hbm.at[vec[target * list_len + l]], buf.at[where, l], sem.at[where]
-            ).start()
+                wide.at[:, half_rows(core, c), :],
+                srcs[c].at[pl.ds(own * other, own)],
+                src_recv.at[c * n_box + other],
+            ).wait()
+
+        for other in range(n_box):
+            here = box != other
+            if other // 2 != 0 or True:
+                here = here & (jnp.logical_not(is_end) | (chip == other // 2))
+            pl.when(here)(functools.partial(arrived, other))
+
+        def swap_one(s, carry):
+            for g in range(size):
+                here = slice(8 * g, 8 * g + 8)
+                swapped[s, here, :] = turn(srcs[c][s, here, :])
             return carry
 
-        lax.fori_loop(0, list_len, one, 0)
-
-    @pl.when(p == 0)
+        first = jnp.where(is_end, 2 * own * chip, 0)
+        last = jnp.where(is_end, 2 * own * chip + 2 * own, n_src)
+        lax.fori_loop(first, last, swap_one, 0)
+
+        @pl.when(helps)
+        def _():
+            def one(p, carry):
+                slot, i = 2 + p // own, lax.rem(p, own)
+                for g, value in enumerate(gather_sum(c, slot, i)):
+                    psend[p, pl.ds(place.start + 8 * g, 8), :] = value
+                return carry
+
+            lax.fori_loop(0, 2 * own, one, 0)
+            p_copy(c, helped).start()
+
+        def one(p, carry):
+            slot, i = p // own, lax.rem(p, own)
+            for g, value in enumerate(gather_sum(c, slot, i)):
+                res[p, pl.ds(place.start + 8 * g, 8), :] = value
+            return carry
+
+        lax.fori_loop(0, 2 * own, one, 0)
+
+    def deliver(c):
+        place = plan.local[c]
+
+        @pl.when(is_end)
+        def _():
+            p_copy(c, chip).wait_recv()
+            res[:, place, :] = res[:, place, :] + precv[:, place, :]
+
+        o_ref[:, half_rows(core, c), :] = res[pl.ds(pl.multiple_of(core * own, 8), own), place, :]
+        result_copy(c).start()
+
+    def chunk_mid(c):
+        one_chunk(c)
+
+        @pl.when(jnp.logical_not(is_end))
+        def _():
+            deliver_plain(c)
+
+    def deliver_plain(c):
+        place = plan.local[c]
+        o_ref[:, half_rows(core, c), :] = res[pl.ds(pl.multiple_of(core * own, 8), own), place, :]
+        result_copy(c).start()
+
+    def deliver_end(c):
+        place = plan.local[c]
+        p_copy(c, chip).wait_recv()
+        res[:, place, :] = res[:, place, :] + precv[:, place, :]
+        deliver_plain(c)
+
+    for c in range(n_chunk):
+        when_has(core, c, lambda c=c: chunk_mid(c))
+
+    @pl.when(is_end)
     def _():
-        fetch(0, 0)
-
-    @pl.when(p + 1 < count)
+        for c in range(n_chunk):
+            when_has(core, c, lambda c=c: deliver_end(c))
+
+    for c in range(n_chunk):
+        when_has(1 - core, c, lambda c=c: result_wait(c).wait_recv())
+        when_has(core, c, lambda c=c: result_copy(c).wait_send())
+        send_chunk(c, lambda copy: copy.wait_send())
+
+        @pl.when(helps)
+        def _():
+            when_has(core, c, lambda: p_copy(c, helped).wait_send())
+
+    to_left.wait_send()
+    to_right.wait_send()
+    list_copy(core, (samp, partner), 0).wait_send()
+
+    @pl.when(is_end)
     def _():
-        fetch(p + 1, 1 - slot)
-
-    @pl.when(p == 0)
-    def _():
-        def one(s, carry):
-            for r in range(0, samples, chunk):
-                here = slice(r, r + chunk)
-                real[s, :, here] = jnp.broadcast_to(x_ref[s, 0:1, here], (2, chunk))
-                imag[s, :, here] = jnp.broadcast_to(x_ref[s, 1:2, here], (2, chunk))
-            return carry
-
-        lax.fori_loop(0, n_src, one, 0)
-
-    def drain(l, carry):
-        pltpu.make_async_copy(t_hbm.at[0], buf.at[slot, l], sem.at[slot]).wait()
-        return carry
-
-    lax.fori_loop(0, list_len, drain, 0)
-
-    def one_chunk(i, carry):
-        r = pl.ds(pl.multiple_of(i * chunk, chunk), chunk)
-        by_real = jnp.zeros((2, chunk), jnp.float32)
-        by_imag = jnp.zeros((2, chunk), jnp.float32)
-        for l in range(list_len):
-            s = src[p * list_len + l]
-            t = buf[slot, l, :, r]
-            by_real = by_real + t * real[s, :, r]
-            by_imag = by_imag + t * imag[s, :, r]
-        o_ref[0, 0:1, r] = by_real[0:1] - by_imag[1:2]
-        o_ref[0, 1:2, r] = by_imag[0:1] + by_real[1:2]
-        return carry
-
-    lax.fori_loop(0, samples // chunk, one_chunk, 0)
-
-
-def pick_chunk(samples):
-    for tiles in (20, 16, 12, 8, 4, 2, 1):
-        if samples % (tiles * LANES) == 0:
-            return tiles * LANES
-    return samples
+        for d in range(2):
+            list_copy(2 + core, (samp, helper * 2 + d), 1 + d).wait_send()
+
+
+class Plan:
+    def __init__(self, n_box, rows, ext_rows, group):
+        self.n_box = n_box
+        self.rows = rows
+        self.padded = -(-rows // 8) * 8
+        groups = self.padded // 8
+        self.split = -(-groups // 2)
+        other = groups - self.split
+        self.sizes = [group] * (other // group)
+        self.sizes += [1] * (self.split - sum(self.sizes))
+        self.starts = [sum(self.sizes[:c]) for c in range(len(self.sizes))]
+        self.both = [self.starts[c] + self.sizes[c] <= other for c in range(len(self.sizes))]
+        self.local = [pl.ds(8 * a, 8 * n) for a, n in zip(self.starts, self.sizes)]
+        self.end_at = (rows - ext_rows) // 8 * 8
+        self.left_rows = self.padded - self.end_at
+        self.left_pad = rows - ext_rows - self.end_at
+        self.right_rows = -(-ext_rows // 8) * 8
+        self.left_at = pl.ds(self.padded, self.left_rows)
+        self.right_at = pl.ds(self.padded + self.left_rows, self.right_rows)
+        self.total = self.padded + self.left_rows + self.right_rows
+        touched = max(self.left_rows, self.right_rows) // 8
+        self.early = sum(self.starts[c] + self.sizes[c] <= other - touched for c in range(len(self.sizes)))
 
 
 def interleave(x):
-    return x.reshape(x.shape[0], 2, -1, LANES).transpose(0, 2, 1, 3).reshape(x.shape[0], -1, LANES)
+    x = x.reshape(x.shape[0], 2, -1, LANES).transpose(0, 2, 1, 3)
+    x = with_layout_constraint(x, Layout(major_to_minor=(0, 1, 2, 3))).reshape(x.shape[0], -1, LANES)
+    return jnp.pad(x, ((0, 0), (0, -x.shape[1] % 8), (0, 0))) if x.shape[1] % 8 else x
+
+
+def separate(x, rows):
+    x = x[:, :rows].reshape(x.shape[0], -1, 2, LANES)
+    x = with_layout_constraint(x, Layout(major_to_minor=(0, 1, 2, 3)))
+    return x.transpose(0, 2, 1, 3).reshape(x.shape[0], 2, -1)
 
 
 def stencil(start, weight, first, low, high, src_low, src_high, n_child):
@@ -236,7 +504,7 @@
 
 
 def per_device(
-    n_samp,
+    n_samp, n_box,
     pattern_a, children_b, children_c, theta_ab, theta_bc,
     phi_start_b, phi_weight_b, phi_start_c, phi_weight_c,
     translation, list_src, list_vec,
@@ -289,16 +557,15 @@
 
     x = interleave(pattern_a)
     steps = pa // 16 if pa % 16 == 0 else 1
-    x = jnp.pad(x, ((0, 0), (0, -x.shape[1] % 8), (0, 0)))
     rows_x = x.shape[1]
     az_step = pa // steps
     tiles = GROUP * theta_c // LANES
-    out_rows = wc // GROUP * 2 * tiles
     ext_rows = ext // GROUP * 2 * tiles
     rows = pc // GROUP * 2 * tiles
+    plan = Plan(n_box, rows, ext_rows, CHUNK)
     one = pl.Buffered(1)
     wide = pl.pallas_call(
-        functools.partial(aggregate_kernel, steps, az_step, wb, wc, out_rows),
+        functools.partial(aggregate_kernel, steps, az_step, wb, wc, ext, plan),
         grid_spec=pltpu.PrefetchScalarGridSpec(
             num_scalar_prefetch=5,
             grid=(steps,),
@@ -311,52 +578,61 @@
                 pl.BlockSpec(s_c.shape, lambda i, *_: (0, 0), pipeline_mode=one),
                 pl.BlockSpec((None,) + phc.shape[1:], lambda i, s, *_: (s[0], 0, 0, 0), pipeline_mode=one),
             ],
-            out_specs=pl.BlockSpec((count_c * out_rows, LANES), lambda i, *_: (0, 0)),
+            out_specs=pl.BlockSpec((count_c * plan.total, LANES), lambda i, *_: (0, 0)),
             scratch_shapes=[
                 pltpu.VMEM((pa, 2 * count_a, LANES), jnp.float32),
                 pltpu.VMEM((wb, 2 * count_b, theta_c), jnp.float32),
             ],
         ),
-        out_shape=jax.ShapeDtypeStruct((count_c * out_rows, LANES), jnp.float32),
+        out_shape=jax.ShapeDtypeStruct((count_c * plan.total, LANES), jnp.float32),
         compiler_params=pltpu.CompilerParams(vmem_limit_bytes=48 << 20),
         name="aggregate",
     )(samp.reshape(1), idx_b, wgt_b, idx_c, wgt_c, x, tab, s_b, phb, tbc, s_c, phc)
-    wide = wide.reshape(count_c, out_rows, LANES)
-    from_left = lax.ppermute(wide[:, out_rows - ext_rows :], "samp", up)
-    from_right = lax.ppermute(wide[:, :ext_rows], "samp", down)
-    zeros = jnp.zeros((count_c, rows - ext_rows, LANES), jnp.float32)
-    mine = (
-        wide[:, ext_rows : out_rows - ext_rows]
-        + jnp.concatenate([from_left, zeros], 1)
-        + jnp.concatenate([zeros, from_right], 1)
-    )
-    mine = mine.reshape(count_c, rows // 2, 2, LANES).transpose(0, 2, 1, 3).reshape(count_c, 2, -1)
-    everyone = lax.all_gather(mine, "box", axis=0, tiled=True)
+    wide = wide.reshape(count_c, plan.total, LANES)
 
     list_len = list_src.shape[1]
-    n_src, _, samples = everyone.shape
-    chunk = pick_chunk(samples)
-    return pl.pallas_call(
-        functools.partial(translate_kernel, list_len, chunk),
-        grid_spec=pltpu.PrefetchScalarGridSpec(
-            num_scalar_prefetch=2,
-            grid=(count_c,),
-            in_specs=[
-                pl.BlockSpec(everyone.shape, lambda i, *_: (0, 0, 0), pipeline_mode=one),
-                pl.BlockSpec(memory_space=pl.ANY),
-            ],
-            out_specs=pl.BlockSpec((1, 2, samples), lambda i, *_: (i, 0, 0)),
-            scratch_shapes=[
-                pltpu.VMEM(everyone.shape, jnp.float32),
-                pltpu.VMEM(everyone.shape, jnp.float32),
-                pltpu.VMEM((2, list_len, 2, samples), jnp.float32),
-                pltpu.SemaphoreType.DMA((2,)),
-            ],
+    n_src = count_c * n_box
+    lists = jnp.concatenate([list_src, list_vec], axis=1)
+    lists = jnp.pad(lists, ((0, 0), (0, -lists.shape[1] % LANES)))
+    t_view = interleave(translation)
+    n_vec = t_view.shape[0]
+    n_chunk = len(plan.sizes)
+    big = 8 * CHUNK
+    half = 8 * plan.split
+    vmem = pl.BlockSpec(memory_space=pltpu.VMEM)
+    out = pl.pallas_call(
+        functools.partial(far_kernel, plan, list_len, n_samp),
+        in_specs=[vmem, vmem, pl.BlockSpec(memory_space=pl.ANY)],
+        out_specs=vmem,
+        scratch_shapes=[
+            pltpu.VMEM((4,) + lists.shape, jnp.int32),
+            pltpu.SMEM((4,) + lists.shape, jnp.int32),
+            pltpu.VMEM((count_c, plan.right_rows, LANES), jnp.float32),
+            pltpu.VMEM((count_c, plan.left_rows, LANES), jnp.float32),
+            pltpu.VMEM((n_src + 8, big, LANES), jnp.float32),
+            pltpu.VMEM((2 * count_c, half, LANES), jnp.float32),
+            pltpu.VMEM((2 * count_c, half, LANES), jnp.float32),
+            pltpu.VMEM((2 * count_c, half, LANES), jnp.float32),
+        ]
+        + [pltpu.VMEM((n_src + 8, 8 * n, LANES), jnp.float32) for n in plan.sizes]
+        + [pltpu.VMEM((n_vec, 8 * n, LANES), jnp.float32) for n in plan.sizes]
+        + [
+            pltpu.SemaphoreType.DMA((7,)),
+            pltpu.SemaphoreType.DMA,
+            pltpu.SemaphoreType.DMA((4,)),
+            pltpu.SemaphoreType.DMA((n_chunk,)),
+            pltpu.SemaphoreType.DMA((n_chunk * n_box,)),
+            pltpu.SemaphoreType.DMA((n_chunk * n_box,)),
+            pltpu.SemaphoreType.DMA((2 * n_chunk,)),
+            pltpu.SemaphoreType.DMA((2 * n_chunk,)),
+        ],
+        out_shape=jax.ShapeDtypeStruct((count_c, plan.padded, LANES), jnp.float32),
+        compiler_params=pltpu.CompilerParams(
+            collective_id=0, has_side_effects=True, vmem_limit_bytes=58 << 20
         ),
-        out_shape=jax.ShapeDtypeStruct((count_c, 2, samples), jnp.float32),
-        compiler_params=pltpu.CompilerParams(vmem_limit_bytes=48 << 20),
-        name="translate",
-    )(list_src.reshape(-1), list_vec.reshape(-1), everyone, translation)
+        name="far",
+    )(wide, lists, t_view)
+    return separate(out, rows)
 
 
 def solution(mesh):
@@ -375,6 +651,6 @@
         P("box", None),
     )
     return jax.shard_map(
-        functools.partial(per_device, mesh.shape["samp"]),
+        functools.partial(per_device, mesh.shape["samp"], mesh.shape["box"]),
         mesh=mesh, in_specs=placed, out_specs=P("box", None, "samp"), check_vma=False,
     )

time: 183 us -> 114 us (0.62)
  waiting for transfers between devices: 71.5 us -> 0.01 us
  Pallas kernels: 59.8 us -> 92.4 us
  local copies, waits for them, and re-layouts: 21.9 us -> 7.23 us
  between operations: 13.6 us -> 0.14 us
  starting transfers between devices: 6.96 us -> 3.93 us
  other arithmetic: 7.52 us -> 9.65 us
    all_gather x1 -> x0, waiting for transfers between devices: 66.2 us -> none  [per_device(): everyone = lax.all_gather(mine, 'box', axis=0, tiled=True)]
    pallas_call x1, Pallas kernels: 18.4 us -> 51.1 us  [per_device(): pl.pallas_call(functools.partial(far_kernel, plan, list_len, n_samp), in_...]
    transpose x1 -> x0, local copies, waits for them, and re-layouts: 8.32 us -> none  [interleave(): x.reshape(x.shape[0], 2, -1, LANES).transpose(0, 2, 1, 3)]
    ppermute x2 -> x0, waiting for transfers between devices: 5.26 us -> none  [the longest x1 3.35 us: per_device(): from_left = lax.ppermute(wide[:, out_rows - ext_rows:], 'samp', up)]
    unnamed x14 -> x6, local copies, waits for them, and re-layouts: 9.14 us -> 4.03 us
    ppermute x2 -> x0, starting transfers between devices: 3.03 us -> none  [the longest x1 2.98 us: per_device(): from_right = lax.ppermute(wide[:, :ext_rows], 'samp', down)]
    ppermute x1, starting transfers between devices: 0.01 us -> 2.97 us  [per_device(): lax.ppermute(jnp.concatenate([table_b[:, pb - near:], table_c[:, pc - nea...]
    ppermute x1, starting transfers between devices: 3.92 us -> 0.96 us  [per_device(): lax.ppermute(jnp.concatenate([table_b[:, :near], table_c[:, :near]], 1),...]
  transfers between devices with their start and end apart: 5 -> 2, of which waited for: 3 -> 0; matrix products, arithmetic and copies ran while one was open for 13% -> 8% of each run, Pallas kernels for 0% -> 0%
where the time goes in v1:
time: 114 us; the launch traced here: 113 us
  Pallas kernels  92.4 us (81%)
  other arithmetic  9.65 us (8%)
  local copies, waits for them, and re-layouts  7.23 us (6%)
  starting transfers between devices  3.93 us (3%)
    pallas_call x1, Pallas kernels, per_device(): pl.pallas_call(functools.partial(far_kernel, plan, list_len, n_samp), in_...  51.1 us
    pallas_call x1, Pallas kernels, per_device(): pl.pallas_call(functools.partial(aggregate_kernel, steps, az_step, wb, wc...  41.3 us
    unnamed x6, local copies, waits for them, and re-layouts  4.03 us
    ppermute x1, starting transfers between devices, per_device(): lax.ppermute(jnp.concatenate([table_b[:, pb - near:], table_c[:, pc - nea...  2.97 us
  transfers between devices with their start and end apart: 2, of which 0 were waited for; matrix products, arithmetic and copies ran while one was open for 8% of the time, Pallas kernels for 0%

profile of v1, /device:TPU:0, one launch (start us, length us, event | category | flops | bytes accessed | tf_op | source)
XLA Modules:
  0.0 113.4 jit_solution(9137075312327744646)
XLA Ops:
  0.0 0.0 copy-start.1
  0.0 0.8 convert_bitcast_fusion.1
  0.8 0.7 convert_bitcast_fusion
  1.5 0.7 pad_maximum_fusion.2
  2.2 0.7 pad_maximum_fusion.3
  2.8 0.1 fusion.14
  2.9 0.1 pad_maximum_fusion.4
  3.0 3.0 %collective-permute-start = (f32[5,16]{1,0:T(8,128)S(1)}, f32[5,16]{1,0:T(8,128)S(1)}, u32[]{:S(2)}, u32[]{:S(2)}) collective-permute-start(f32[5,16]{1,0:T(8,128)S(1)} %pad_maximum_fusion.4), channel_id=1, source_target_pairs={{0,8},{8,16},{16,24},{24,0},{1,9},{9,17},{17,25},{25,1},{2,10},{10... | collective-permute-start | bytes 968 | tf_op jit(solution)/shard_map/ppermute | solution.py:532
  6.0 0.1 pad_maximum_fusion.5
  6.0 1.0 collective-permute-start.1
  7.0 0.9 reduce_precision.11
  7.9 1.0 copy.20
  8.9 0.9 fusion.13
  9.8 0.1 copy.19
  9.9 0.7 compare_bitcast_fusion.1
  10.6 0.7 subtract_bitcast_fusion.1
  11.3 0.1 eq.34
  11.4 0.1 ge.44
  11.5 0.1 fusion.6
  11.6 0.7 compare_bitcast_fusion
  12.3 0.7 subtract_bitcast_fusion
  13.0 0.1 copy.22
  13.1 0.1 eq.38
  13.2 0.1 copy.23
  13.3 0.1 ge.48
  13.3 0.1 fusion.7
  13.4 0.1 add_convert_fusion.1.sc_ref
  13.5 0.8 constant_dynamic-update-slice_fusion.1
  14.3 0.1 fusion.4
  14.5 0.1 pad_maximum_fusion.tab_ref
  14.7 0.8 pad_add_fusion
  15.4 0.6 pad.6.lists
  16.0 0.0 collective-permute-done
  16.0 0.1 slice.44
  16.1 0.0 collective-permute-done.1
  16.1 0.1 slice.45
  16.2 0.8 pad_maximum_fusion.7
  17.0 0.1 slice.38
  17.1 0.8 pad_maximum_fusion.6
  17.9 0.0 copy-done.1
  17.9 41.3 %aggregate.1 = f32[1984,128]{1,0:T(8,128)S(1)} custom-call(s32[1]{0:T(128)} %bitcast.samp, s32[4,69]{1,0:T(4,128)S(1)} %broadcast_clamp_fusion.idx_b, f32[4,69]{1,0:T(4,128)S(1)} %slice_select_fusion.1.wgt_b, s32[4,96]{1,0:T(4,128)S(1)} %add_clamp_fusion.idx_c, f32[4,96]{1,0:T(4,128)S(1)} %slice_select_fusion.wgt_c, f32[128,72,128]{2,1,0:T(8,128)} %bitcast.52, ...), custom_call_target="tpu_custom_call" | custom-call | tf_op jit(solution)/shard_map/aggregate/pallas_call | solution.py:567
  59.2 0.0 copy-start
  59.2 1.0 copy-done
  60.2 51.1 %far.1 = f32[8,200,128]{2,1,0:T(8,128)} custom-call(f32[8,248,128]{2,1,0:T(8,128)} %bitcast.50, s32[8,128]{1,0:T(8,128)} %pad.6.lists, f32[316,200,128]{2,1,0:T(8,128)} %bitcast.51), custom_call_target="tpu_custom_call" | custom-call | tf_op jit(solution)/shard_map/far/pallas_call | solution.py:603
  111.3 2.1 %copy.27 = f32[8,2,12800]{2,1,0:T(2,128)} copy(f32[8,2,12800]{2,1,0:T(2,128)} %bitcast.53) | data formatting | bytes 1638400
  (12 shorter events, 0.3 us)
Async XLA Ops:
  0.0 17.9 %copy-start.1 = (f32[4,69,16,128]{3,2,1,0:T(8,128)S(1)}, f32[4,69,16,128]{3,2,1,0:T(8,128)}, u32[]{:S(2)}) copy-start(f32[4,69,16,128]{3,2,1,0:T(8,128)} %constant.96.clone.phb_ref) | copy-start | bytes 6782980
  3.0 13.0 %collective-permute-start = (f32[5,16]{1,0:T(8,128)S(1)}, f32[5,16]{1,0:T(8,128)S(1)}, u32[]{:S(2)}, u32[]{:S(2)}) collective-permute-start(f32[5,16]{1,0:T(8,128)S(1)} %pad_maximum_fusion.4), channel_id=1, source_target_pairs={{0,8},{8,16},{16,24},{24,0},{1,9},{9,17},{17,25},{25,1},{2,10},{10... | collective-permute-start | bytes 968 | tf_op jit(solution)/shard_map/ppermute | solution.py:532
  6.0 10.1 %collective-permute-start.1 = (f32[5,16]{1,0:T(8,128)S(1)}, f32[5,16]{1,0:T(8,128)S(1)}, u32[]{:S(2)}, u32[]{:S(2)}) collective-permute-start(f32[5,16]{1,0:T(8,128)S(1)} %pad_maximum_fusion.5), channel_id=1, source_target_pairs={{8,0},{16,8},{24,16},{0,24},{9,1},{17,9},{25,17},{1,25},{10,2},{18... | collective-permute-start | bytes 968 | tf_op jit(solution)/shard_map/ppermute | solution.py:533
  59.2 1.0 copy-start

commit v2 on v1

v2 whole, which is shorter than its diff:
```python
import functools

import jax
import jax.numpy as jnp
import numpy as np
from jax import lax
from jax.experimental import pallas as pl
from jax.experimental.layout import Layout, with_layout_constraint
from jax.experimental.pallas import tpu as pltpu
from jax.sharding import PartitionSpec as P

SIZE_B = 8
SIZE_C = 16
LANES = 128
MESH = pl.DeviceIdType.MESH
GROUP = 4
FIRST_CHUNKS = (2, 4, 4, 2, 1)
REPS = ((1, 1), (1, -1), (-1, 1), (-1, -1))


def window(first, last, n_child, n_parent):
    low = 0
    while (low - 1) * n_child // n_parent + 2 >= first:
        low -= 1
    high = 0
    while (high + 1) * n_child // n_parent - 2 <= last:
        high += 1
    return low, high + 1


def quarters(parts):
    return parts // 4 if parts % 4 == 0 else parts


def phase_table(parts, per_part, low, high, n_theta, size):
    n_phi = parts * per_part
    theta = np.pi * (np.arange(n_theta) + 0.5) / n_theta
    first = np.arange(quarters(parts))[:, None] * per_part
    phi = 2.0 * np.pi * (first + np.arange(low, high)[None]) / n_phi
    u_x = np.cos(phi)[..., None] * np.sin(theta)
    u_y = np.sin(phi)[..., None] * np.sin(theta)
    u_z = np.broadcast_to(np.cos(theta), u_x.shape)
    psi = np.stack([0.5 * np.pi * size * (s_x * u_x + s_y * u_y + u_z) for s_x, s_y in REPS], axis=2)
    return np.concatenate([np.cos(psi), np.sin(psi)], axis=2).astype(np.float32)


def octant(rep, turns):
    s_x, s_y = REPS[rep]
    for _ in range(turns):
        s_x, s_y = -s_y, s_x
    return 2 * (s_x + 1) + (s_y + 1) + 1


def split(x):
    high = x.astype(jnp.bfloat16)
    return high, (x - high.astype(jnp.float32)).astype(jnp.bfloat16)


def mm(a, b):
    return jnp.dot(a, b, preferred_element_type=jnp.float32)


def pick(index, values):
    out = jnp.int32(values[0])
    for k in range(1, len(values)):
        out = jnp.where(index == k, values[k], out)
    return out


class Plan:
    def __init__(self, n_samp, n_box, pa, pb, pc, theta_c):
        self.n_samp, self.n_box = n_samp, n_box
        self.pa, self.pb, self.pc = pa, pb, pc
        n_a, n_b, n_c = n_samp * pa, n_samp * pb, n_samp * pc
        self.low_b, self.high_b = window(0, pa - 1, n_a, n_b)
        low_c, high_c = window(self.low_b, self.high_b - 1, n_b, n_c)
        self.ext = -(-max(-low_c, high_c - pc) // GROUP) * GROUP
        self.low_c, self.high_c = -self.ext, pc + self.ext
        self.wb, self.wc = self.high_b - self.low_b, self.high_c - self.low_c
        self.unit_rows = 2 * GROUP * theta_c // LANES
        self.edge, self.inner = self.ext // GROUP, pc // GROUP
        self.rows = rows = self.inner * self.unit_rows
        ext_rows = self.edge * self.unit_rows
        self.padded = -(-rows // 8) * 8
        groups = self.padded // 8
        self.split = -(-groups // 2)
        other = groups - self.split
        self.sizes = []
        for size in FIRST_CHUNKS + (1,) * self.split:
            left = other - sum(self.sizes)
            if sum(self.sizes) < self.split:
                self.sizes.append(min(size, left) if left > 0 else 1)
        self.starts = [sum(self.sizes[:c]) for c in range(len(self.sizes))]
        ends = [a + n for a, n in zip(self.starts, self.sizes)]
        self.both = [end <= other for end in ends]
        self.local = [pl.ds(8 * a, 8 * n) for a, n in zip(self.starts, self.sizes)]
        self.end_at = (rows - ext_rows) // 8 * 8
        self.left_rows = self.padded - self.end_at
        self.left_pad = rows - ext_rows - self.end_at
        self.right_rows = -(-ext_rows // 8) * 8
        self.left_at = pl.ds(self.padded, self.left_rows)
        self.right_at = pl.ds(self.padded + self.left_rows, self.right_rows)
        self.total = self.padded + self.left_rows + self.right_rows
        touched = max(self.left_rows, self.right_rows) // 8
        self.early = sum(end <= other - touched for end in ends)
        c_low, c_high, b_low, b_high, a_low, a_high = [], [], [], [], [], []
        for c in range(self.early + 1):
            first, last = 0, self.edge * 2 + self.inner
            if c < self.early:
                first = self.edge + 8 * (self.split - ends[c]) // self.unit_rows
                last = min(last, self.edge - (-8 * (self.split + ends[c]) // self.unit_rows))
            c_low.append(first)
            c_high.append(last)
            b0, b1 = 0, self.wb
            if c < self.early:
                b0 = (self.low_c + GROUP * first) * n_b // n_c - 2 - self.low_b
                b1 = (self.low_c + GROUP * last - 1) * n_b // n_c + 3 - self.low_b
                b0, b1 = max(b0, 0), min(b1, self.wb)
            b_low.append(b0)
            b_high.append(b1)
            a0 = max((b0 + self.low_b) * n_a // n_b - 2, 0)
            a1 = min((b1 - 1 + self.low_b) * n_a // n_b + 3, pa)
            if c == self.early:
                a0, a1 = 0, pa
            a_low.append(a0 // GROUP)
            a_high.append(-(-a1 // GROUP))
        self.levels = (self.spans(a_low, a_high), self.spans(b_low, b_high), self.spans(c_low, c_high))

    @staticmethod
    def spans(low, high):
        before_low, before_high = [high[0]] + low[:-1], [high[0]] + high[:-1]
        left = [b - a for a, b in zip(low, before_low)]
        count = [n + b - a for n, a, b in zip(left, before_high, high)]
        return low, left, before_high, count


def stencil(plan, samp, start, weight):
    row = lax.broadcasted_iota(jnp.int32, start.shape, 0)
    at_b = row < 4
    n_a, n_b = plan.n_samp * plan.pa, plan.n_samp * plan.pb

    def choose(b, c):
        return jnp.where(at_b, b, c)

    tap = start + choose(row - samp * plan.pa, row - 4 - samp * plan.pb)
    count, half = choose(n_a, n_b), choose(n_a // 2, n_b // 2)
    low, high = choose(0, plan.low_b), choose(plan.pa, plan.high_b)
    centre = choose(plan.pa // 2, (plan.low_b + plan.high_b) // 2)
    for _ in range(2):
        tap = jnp.where(tap - centre > half, tap - count, tap)
        tap = jnp.where(tap - centre < -half, tap + count, tap)
    inside = (tap >= low) & (tap < high)
    return jnp.clip(tap - low, 0, high - low - 1), jnp.where(inside, weight, 0.0)


def far_kernel(
    plan, list_len,
    x_hbm, theta_ab, theta_bc, child_b, child_c, start_b, weight_b, start_c, weight_c,
    phb_hbm, phc_hbm, src_ref, vec_ref, t_hbm, o_ref,
    x_ref, grid_a, grid_b, phb, phc, tab, tbc, s_b, s_c, ints, floats, tables_i, tables_w, idx, wgt, wide,
    lists, list_all, list_smem, halo_left, halo_right, swapped, res, psend, precv, *rest,
):
    n_chunk = len(plan.sizes)
    srcs, tbufs = rest[:n_chunk], rest[n_chunk : 2 * n_chunk]
    (in_sem, table_sem, list_sem, smem_sem, halo_sem, t_sem, src_send, src_recv, p_sem, out_sem) = rest[2 * n_chunk :]
    samp, box = lax.axis_index("samp"), lax.axis_index("box")
    n_box, n_samp = plan.n_box, plan.n_samp
    n_chip = n_box // 2
    chip, core = box // 2, box % 2
    partner = chip * 2 + 1 - core
    own = wide.shape[0]
    first_end, last_end = chip == 0, chip == n_chip - 1
    is_end = first_end | last_end
    helps_first, helps_last = chip == 1, chip == n_chip - 2
    helps = helps_first | helps_last
    helped = jnp.where(helps_first, 0, n_chip - 1)
    helper = jnp.where(first_end, 1, n_chip - 2)
    left = (lax.rem(samp + n_samp - 1, n_samp), box)
    right = (lax.rem(samp + 1, n_samp), box)
    n_base = quarters(n_samp)

    in_copies = [
        pltpu.make_async_copy(x_hbm, x_ref, in_sem.at[0]),
        pltpu.make_async_copy(phb_hbm.at[lax.rem(samp, n_base)], phb, in_sem.at[1]),
        pltpu.make_async_copy(phc_hbm.at[lax.rem(samp, n_base)], phc, in_sem.at[2]),
    ]
    for copy in in_copies:
        copy.start()

    count_a, count_b, count_c = x_ref.shape[0], child_b.shape[0], child_c.shape[0]
    theta_a, theta_b = theta_ab.shape
    theta_c = theta_bc.shape[1]
    ints[1, 0:1, 0 : plan.pb] = start_b[...]
    ints[1, 1:2, 0 : plan.pc] = start_c[...]
    floats[1, 0:4, 0 : plan.pb] = weight_b[...]
    floats[1, 4:8, 0 : plan.pc] = weight_c[...]
    lists[:, 0:list_len] = src_ref[...]
    lists[:, list_len : 2 * list_len] = vec_ref[...]

    def remote(src, dst, send, recv, device):
        return pltpu.make_async_remote_copy(
            src_ref=src, dst_ref=dst, send_sem=send, recv_sem=recv, device_id=device, device_id_type=MESH
        )

    barrier = pltpu.get_barrier_semaphore()
    for other in range(n_box):
        @pl.when(box != other)
        def _():
            pl.semaphore_signal(barrier, inc=1, device_id=(samp, other), device_id_type=MESH)
    for device in (left, right):
        pl.semaphore_signal(barrier, inc=1, device_id=device, device_id_type=MESH)

    tab[...] = jnp.zeros(tab.shape, jnp.bfloat16)
    high, low = split(theta_ab[...])
    for pair in range(2):
        at = pair * (2 * theta_a - LANES)
        for k in range(2):
            rows = slice(at + k * theta_a, at + (k + 1) * theta_a)
            cols = slice(k * theta_b, (k + 1) * theta_b)
            tab[pair, 0, rows, cols] = high
            tab[pair, 1, rows, cols] = low
    high, low = split(theta_bc[...])
    tbc[0, :theta_b] = high
    tbc[0, theta_b:] = high
    tbc[1, :theta_b] = low
    tbc[1, theta_b:] = low
    turns = samp // n_base

    def one_hot(child, first, count):
        ids = child[...]
        lane = lax.broadcasted_iota(jnp.int32, (ids.shape[0], count), 1) + first
        plus, minus = [], []
        for rep in range(4):
            hots = []
            for flip in range(2):
                column = None
                for t in range(n_samp // n_base):
                    o = octant(rep, t)
                    o = 7 - o if flip else o
                    here = ids[:, o : o + 1]
                    column = here if column is None else jnp.where(turns == t, here, column)
                hots.append(jnp.where(column == lane, 1.0, 0.0))
            plus.append(hots[0] + hots[1])
            minus.append(hots[0] - hots[1])
        hot = jnp.concatenate(plus + minus, axis=0).astype(jnp.bfloat16)
        return jnp.concatenate([hot, hot], axis=1)

    s_b[...] = one_hot(child_b, box * count_a, count_a)
    s_c[...] = one_hot(child_c, box * count_b, count_b)
    wide[...] = jnp.zeros(wide.shape, jnp.float32)
    pl.semaphore_wait(barrier, n_box + 1)

    table_copies = []
    for k, ref in enumerate((ints, floats)):
        for d, (slot, device) in enumerate(((2, left), (0, right))):
            n = 4 * k + 2 * d
            table_copies.append(remote(ref.at[1], ref.at[slot], table_sem.at[n], table_sem.at[n + 1], device))
    for copy in table_copies:
        copy.start()

    def half_rows(which, c):
        count = 8 * plan.sizes[c]
        low = 8 * (plan.split - plan.starts[c]) - count
        high = 8 * (plan.split + plan.starts[c])
        return pl.ds(pl.multiple_of(jnp.where(which == 0, low, high), 8), count)

    def has(which, c):
        return (which == 0) | plan.both[c]

    def t_copy(c):
        return pltpu.make_async_copy(t_hbm.at[:, half_rows(core, c), :], tbufs[c], t_sem.at[c])

    def when_has(which, c, do):
        if plan.both[c]:
            do()
        else:
            pl.when(which == 0)(do)

    to_left = remote(wide.at[:, plan.left_at, :], halo_right, halo_sem.at[0], halo_sem.at[1], left)
    to_right = remote(wide.at[:, plan.right_at, :], halo_left, halo_sem.at[2], halo_sem.at[3], right)

    def list_copy(slot, device, k):
        return remote(lists, list_all.at[slot], list_sem.at[k], list_sem.at[3 + slot], device)

    list_copy(core, (samp, partner), 0).start()

    @pl.when(is_end)
    def _():
        for d in range(2):
            list_copy(2 + core, (samp, helper * 2 + d), 1 + d).start()

    def src_copy(c, chip_to, d):
        index = c * n_box + chip_to * 2 + d
        return remote(
            wide.at[:, half_rows(d, c), :],
            srcs[c].at[pl.ds(pl.multiple_of(own * box, 8), own)],
            src_send.at[index],
            src_recv.at[c * n_box + box],
            (samp, chip_to * 2 + d),
        )

    def send_chunk(c, act):
        def to_partner():
            act(src_copy(c, chip, 1 - core))

        when_has(1 - core, c, to_partner)
        for chip_to in range(1, n_chip - 1):
            @pl.when(chip != chip_to)
            def _():
                for d in range(2):
                    if d == 0 or plan.both[c]:
                        act(src_copy(c, chip_to, d))

    for c in range(n_chunk):
        when_has(core, c, lambda c=c: t_copy(c).start())
    list_all[core] = lists[...]

    x_rows = x_ref.reshape(count_a * x_ref.shape[1], LANES)
    wide_rows = wide.reshape(own * plan.total, LANES)
    stride_x = x_ref.shape[1]

    def theta_block(q):
        highs, lows = [], []
        for c in range(2):
            tiles = [split(x_rows[pl.ds(6 * q + 2 * j + c, count_a, stride=stride_x), :]) for j in range(3)]
            highs.append([t[0] for t in tiles])
            lows.append([t[1] for t in tiles])
        for pair in range(2):
            here = slice(pair, pair + 2)
            high = jnp.concatenate([jnp.concatenate(h[here], axis=1) for h in highs], axis=0)
            low = jnp.concatenate([jnp.concatenate(h[here], axis=1) for h in lows], axis=0)
            both = mm(high, tab[pair, 0]) + mm(low, tab[pair, 0]) + mm(high, tab[pair, 1])
            for k in range(2):
                grid_a[GROUP * q + 2 * pair + k] = both[:, k * LANES : (k + 1) * LANES]

    def taps(n, per_part, first_row):
        part = jnp.where(n >= 0, 1, 0) + jnp.where(n >= per_part, 1, 0)
        col = n + per_part * (1 - part)
        return [(idx[part, first_row + k, col], wgt[part, first_row + k, col]) for k in range(4)]

    def octants(phase, plus_r, plus_i, minus_r, minus_i, count):
        real = imag = None
        for j in range(4):
            cosine, sine = phase[j : j + 1, :], phase[4 + j : 5 + j, :]
            here = slice(j * count, (j + 1) * count)
            re = plus_r[here] * cosine - minus_i[here] * sine
            im = plus_i[here] * cosine + minus_r[here] * sine
            real, imag = (re, im) if real is None else (real + re, imag + im)
        return real, imag

    def level_b(m):
        stencil_b = taps(m + plan.low_b, plan.pb, 0)
        parts = []
        for c in range(2):
            here = slice(c * count_a, (c + 1) * count_a)
            value = None
            for at, weight in stencil_b:
                term = weight * grid_a[at, here, :]
                value = term if value is None else value + term
            parts.append(split(value))
        stacked = jnp.concatenate(
            [
                jnp.concatenate([parts[0][0], parts[1][0]], axis=1),
                jnp.concatenate([parts[0][1], parts[1][1]], axis=1),
            ],
            axis=0,
        )
        picked = mm(s_b[...], stacked)
        mid = 4 * count_b
        real, imag = octants(
            phb[m], picked[:mid, :LANES], picked[:mid, LANES:], picked[mid:, :LANES], picked[mid:, LANES:], count_b
        )
        high, low = split(jnp.concatenate([real, imag], axis=0))
        both = jnp.concatenate([high, low], axis=1)
        return mm(both, tbc[0]) + mm(high, tbc[1, :LANES])

    def level_c(g):
        reals, imags = [], []
        for i in range(GROUP):
            n = g * GROUP + i
            value = None
            for at, weight in taps(n + plan.low_c, plan.pc, 4):
                term = weight * grid_b[at]
                value = term if value is None else value + term
            high, low = split(value)
            rr = mm(s_c[...], jnp.concatenate([high[:count_b], low[:count_b]], axis=0))
            ri = mm(s_c[...], jnp.concatenate([high[count_b:], low[count_b:]], axis=0))
            mid = 4 * count_c
            real, imag = octants(phc[n], rr[:mid], ri[:mid], rr[mid:], ri[mid:], count_c)
            reals.append(real)
            imags.append(imag)
        base = jnp.where(
            g < plan.edge,
            plan.padded + plan.left_pad + g * plan.unit_rows,
            jnp.where(
                g < plan.edge + plan.inner,
                (g - plan.edge) * plan.unit_rows,
                plan.padded + plan.left_rows + (g - plan.edge - plan.inner) * plan.unit_rows,
            ),
        )
        for c, flat in enumerate((jnp.concatenate(reals, axis=1), jnp.concatenate(imags, axis=1))):
            for t in range(plan.unit_rows // 2):
                wide_rows[pl.ds(base + 2 * t + c, own, stride=plan.total), :] = flat[:, t * LANES : (t + 1) * LANES]

    for copy in table_copies:
        copy.wait_recv()
    for part in range(3):
        row = lax.broadcasted_iota(jnp.int32, ints.shape[1:], 0)
        start = jnp.where(row < 4, ints[part, 0:1, :], ints[part, 1:2, :])
        at, weight = stencil(plan, samp, start, floats[part])
        tables_i[part] = at
        tables_w[part] = weight
    to_idx = pltpu.make_async_copy(tables_i, idx, in_sem.at[3])
    to_wgt = pltpu.make_async_copy(tables_w, wgt, in_sem.at[4])
    to_idx.start()
    to_wgt.start()
    to_idx.wait()
    to_wgt.wait()
    for copy in in_copies:
        copy.wait()

    def phase(ph, carry):
        def items(level):
            low, before, after, count = (pick(ph, values) for values in plan.levels[level])
            return count, lambda i: jnp.where(i < before, low + i, after + i - before)

        count, item = items(0)

        def one_a(i, carry):
            theta_block(item(i))
            return carry

        lax.fori_loop(0, count, one_a, 0)
        count_m, item_m = items(1)

        def two_b(i, carry):
            m0, m1 = item_m(2 * i), item_m(jnp.minimum(2 * i + 1, count_m - 1))
            v0, v1 = level_b(m0), level_b(m1)
            grid_b[m0] = v0
            grid_b[m1] = v1
            return carry

        lax.fori_loop(0, pick(ph, [-(-n // 2) for n in plan.levels[1][3]]), two_b, 0)
        count_g, item_g = items(2)

        def one_c(i, carry):
            level_c(item_g(i))
            return carry

        lax.fori_loop(0, count_g, one_c, 0)
        for c in range(plan.early):
            @pl.when(ph == c)
            def _():
                send_chunk(c, lambda copy: copy.start())

        return carry

    lax.fori_loop(0, plan.early + 1, phase, 0)
    to_left.start()
    to_right.start()

    def finish_edges():
        to_left.wait_recv()
        to_right.wait_recv()
        at_end = pl.ds(plan.end_at, halo_right.shape[1])
        wide[:, at_end, :] = wide[:, at_end, :] + halo_right[...]
        at_start = pl.ds(0, halo_left.shape[1])
        wide[:, at_start, :] = wide[:, at_start, :] + halo_left[...]
        for c in range(plan.early, n_chunk):
            send_chunk(c, lambda copy: copy.start())

    list_copy(1 - core, (samp, partner), 0).wait_recv()

    @pl.when(helps)
    def _():
        for d in range(2):
            list_copy(2 + d, (samp, partner), 0).wait_recv()

    n_src = own * n_box
    low = jnp.where(last_end, n_src - 2 * own, 0)
    high = jnp.where(first_end, 2 * own, n_src)
    low_p = jnp.where(helps_first, 2 * own, 0)
    high_p = jnp.where(helps_last, n_src - 2 * own, n_src)
    lane = lax.broadcasted_iota(jnp.int32, list_all.shape[1:], 1)
    for slot in range(4):
        a, b = (low, high) if slot < 2 else (low_p, high_p)
        value = list_all[slot]
        gone = (lane < list_len) & ((value < a) | (value >= b))
        list_all[slot] = jnp.where(gone, n_src, value)
    to_smem = pltpu.make_async_copy(list_all, list_smem, smem_sem)
    to_smem.start()
    to_smem.wait()

    even = lax.rem(lax.broadcasted_iota(jnp.int32, (8, LANES), 0), 2) == 0

    def turn(x):
        return jnp.where(even, pltpu.roll(x, 7, 0), pltpu.roll(x, 1, 0))

    def gather_sum(c, slot, i):
        size = plan.sizes[c]
        by_same = [jnp.zeros((8, LANES), jnp.float32) for _ in range(size)]
        by_turned = [jnp.zeros((8, LANES), jnp.float32) for _ in range(size)]
        for l in range(list_len):
            s = list_smem[slot, i, l]
            v = list_smem[slot, i, list_len + l]
            for g in range(size):
                here = slice(8 * g, 8 * g + 8)
                t = tbufs[c][v, here, :]
                by_same[g] = by_same[g] + t * srcs[c][s, here, :]
                by_turned[g] = by_turned[g] + t * swapped[s, here, :]
        out = []
        for g in range(size):
            x, y = by_same[g], by_turned[g]
            out.append(jnp.where(even, x - pltpu.roll(x, 7, 0), y + pltpu.roll(y, 1, 0)))
        return out

    def result_copy(c):
        return remote(
            res.at[pl.ds(pl.multiple_of((1 - core) * own, 8), own), plan.local[c], :],
            o_ref.at[:, half_rows(core, c), :],
            out_sem.at[c],
            out_sem.at[n_chunk + c],
            (samp, partner),
        )

    def result_wait(c):
        return remote(
            res.at[pl.ds(pl.multiple_of((1 - core) * own, 8), own), plan.local[c], :],
            o_ref.at[:, half_rows(1 - core, c), :],
            out_sem.at[c],
            out_sem.at[n_chunk + c],
            (samp, partner),
        )

    def p_copy(c, chip_to):
        return remote(
            psend.at[:, plan.local[c], :],
            precv.at[:, plan.local[c], :],
            p_sem.at[c],
            p_sem.at[n_chunk + c],
            (samp, chip_to * 2 + core),
        )

    def one_chunk(c):
        size = plan.sizes[c]
        rows = 8 * size
        place = plan.local[c]
        srcs[c][pl.ds(pl.multiple_of(own * box, 8), own)] = wide[:, half_rows(core, c), :]
        srcs[c][pl.ds(n_src, 8)] = jnp.zeros((8, rows, LANES), jnp.float32)
        swapped[pl.ds(n_src, 8)] = jnp.zeros((8, swapped.shape[1], LANES), jnp.float32)
        t_copy(c).wait()

        def arrived(other):
            pltpu.make_async_copy(
                wide.at[:, half_rows(core, c), :],
                srcs[c].at[pl.ds(own * other, own)],
                src_recv.at[c * n_box + other],
            ).wait()

        for other in range(n_box):
            here = (box != other) & (jnp.logical_not(is_end) | (chip == other // 2))
            pl.when(here)(functools.partial(arrived, other))

        def swap_one(s, carry):
            for g in range(size):
                here = slice(8 * g, 8 * g + 8)
                swapped[s, here, :] = turn(srcs[c][s, here, :])
            return carry

        first = jnp.where(is_end, 2 * own * chip, 0)
        last = jnp.where(is_end, 2 * own * chip + 2 * own, n_src)
        lax.fori_loop(first, last, swap_one, 0)

        @pl.when(helps)
        def _():
            def one(p, carry):
                slot, i = 2 + p // own, lax.rem(p, own)
                for g, value in enumerate(gather_sum(c, slot, i)):
                    psend[p, pl.ds(place.start + 8 * g, 8), :] = value
                return carry

            lax.fori_loop(0, 2 * own, one, 0)
            p_copy(c, helped).start()

        def one(p, carry):
            slot, i = p // own, lax.rem(p, own)
            for g, value in enumerate(gather_sum(c, slot, i)):
                res[p, pl.ds(place.start + 8 * g, 8), :] = value
            return carry

        lax.fori_loop(0, 2 * own, one, 0)

    def chunk_mid(c):
        one_chunk(c)

        @pl.when(jnp.logical_not(is_end))
        def _():
            deliver_plain(c)

    def deliver_plain(c):
        place = plan.local[c]
        o_ref[:, half_rows(core, c), :] = res[pl.ds(pl.multiple_of(core * own, 8), own), place, :]
        result_copy(c).start()

    def deliver_end(c):
        place = plan.local[c]
        p_copy(c, chip).wait_recv()
        res[:, place, :] = res[:, place, :] + precv[:, place, :]
        deliver_plain(c)

    for c in range(n_chunk):
        if c == min(1, plan.early):
            finish_edges()
        when_has(core, c, lambda c=c: chunk_mid(c))

    @pl.when(is_end)
    def _():
        for c in range(n_chunk):
            when_has(core, c, lambda c=c: deliver_end(c))

    for c in range(n_chunk):
        when_has(1 - core, c, lambda c=c: result_wait(c).wait_recv())
        when_has(core, c, lambda c=c: result_copy(c).wait_send())
        send_chunk(c, lambda copy: copy.wait_send())

        @pl.when(helps)
        def _():
            when_has(core, c, lambda: p_copy(c, helped).wait_send())

    for copy in table_copies:
        copy.wait_send()
    to_left.wait_send()
    to_right.wait_send()
    list_copy(core, (samp, partner), 0).wait_send()

    @pl.when(is_end)
    def _():
        for d in range(2):
            list_copy(2 + core, (samp, helper * 2 + d), 1 + d).wait_send()


def interleave(x):
    x = x.reshape(x.shape[0], 2, -1, LANES).transpose(0, 2, 1, 3)
    x = with_layout_constraint(x, Layout(major_to_minor=(0, 1, 2, 3))).reshape(x.shape[0], -1, LANES)
    return jnp.pad(x, ((0, 0), (0, -x.shape[1] % 8), (0, 0))) if x.shape[1] % 8 else x


def separate(x, rows):
    x = x[:, :rows].reshape(x.shape[0], -1, 2, LANES)
    x = with_layout_constraint(x, Layout(major_to_minor=(0, 1, 2, 3)))
    return x.transpose(0, 2, 1, 3).reshape(x.shape[0], 2, -1)


def per_device(
    n_samp, n_box,
    pattern_a, children_b, children_c, theta_ab, theta_bc,
    phi_start_b, phi_weight_b, phi_start_c, phi_weight_c,
    translation, list_src, list_vec,
):
    count_a, count_b, count_c = pattern_a.shape[0], children_b.shape[0], children_c.shape[0]
    theta_a, theta_b = theta_ab.shape
    theta_c = theta_bc.shape[1]
    pa = pattern_a.shape[2] // theta_a
    plan = Plan(n_samp, n_box, pa, phi_start_b.shape[0], phi_start_c.shape[0], theta_c)
    phb = jnp.asarray(phase_table(n_samp, plan.pb, plan.low_b, plan.high_b, theta_b, SIZE_B))
    phc = jnp.asarray(phase_table(n_samp, plan.pc, plan.low_c, plan.high_c, theta_c, SIZE_C))
    x = interleave(pattern_a)
    t_view = interleave(translation)
    list_len = list_src.shape[1]
    n_src = count_c * n_box
    n_chunk = len(plan.sizes)
    big = 8 * max(plan.sizes)
    half = 8 * plan.split
    list_lanes = -(-2 * list_len // LANES) * LANES
    lanes = -(-max(plan.pb, plan.pc) // LANES) * LANES
    vmem = pl.BlockSpec(memory_space=pltpu.VMEM)
    hbm = pl.BlockSpec(memory_space=pl.ANY)
    f32, bf16, i32 = jnp.float32, jnp.bfloat16, jnp.int32
    out = pl.pallas_call(
        functools.partial(far_kernel, plan, list_len),
        in_specs=[hbm] + [vmem] * 8 + [hbm] * 2 + [vmem] * 2 + [hbm],
        out_specs=vmem,
        scratch_shapes=[
            pltpu.VMEM(x.shape, f32),
            pltpu.VMEM((pa, 2 * count_a, LANES), f32),
            pltpu.VMEM((plan.wb, 2 * count_b, theta_c), f32),
            pltpu.VMEM(phb.shape[1:], f32),
            pltpu.VMEM(phc.shape[1:], f32),
            pltpu.VMEM((2, 2, 2 * LANES, 2 * theta_b), bf16),
            pltpu.VMEM((2, 2 * theta_b, theta_c), bf16),
            pltpu.VMEM((8 * count_b, 2 * count_a), bf16),
            pltpu.VMEM((8 * count_c, 2 * count_b), bf16),
            pltpu.VMEM((3, 8, lanes), i32),
            pltpu.VMEM((3, 8, lanes), f32),
            pltpu.VMEM((3, 8, lanes), i32),
            pltpu.VMEM((3, 8, lanes), f32),
            pltpu.SMEM((3, 8, lanes), i32),
            pltpu.SMEM((3, 8, lanes), f32),
            pltpu.VMEM((count_c, plan.total, LANES), f32),
            pltpu.VMEM((count_c, list_lanes), i32),
            pltpu.VMEM((4, count_c, list_lanes), i32),
            pltpu.SMEM((4, count_c, list_lanes), i32),
            pltpu.VMEM((count_c, plan.right_rows, LANES), f32),
            pltpu.VMEM((count_c, plan.left_rows, LANES), f32),
            pltpu.VMEM((n_src + 8, big, LANES), f32),
            pltpu.VMEM((2 * count_c, half, LANES), f32),
            pltpu.VMEM((2 * count_c, half, LANES), f32),
            pltpu.VMEM((2 * count_c, half, LANES), f32),
        ]
        + [pltpu.VMEM((n_src + 8, 8 * n, LANES), f32) for n in plan.sizes]
        + [pltpu.VMEM((t_view.shape[0], 8 * n, LANES), f32) for n in plan.sizes]
        + [
            pltpu.SemaphoreType.DMA((5,)),
            pltpu.SemaphoreType.DMA((8,)),
            pltpu.SemaphoreType.DMA((7,)),
            pltpu.SemaphoreType.DMA,
            pltpu.SemaphoreType.DMA((4,)),
            pltpu.SemaphoreType.DMA((n_chunk,)),
            pltpu.SemaphoreType.DMA((n_chunk * n_box,)),
            pltpu.SemaphoreType.DMA((n_chunk * n_box,)),
            pltpu.SemaphoreType.DMA((2 * n_chunk,)),
            pltpu.SemaphoreType.DMA((2 * n_chunk,)),
        ],
        out_shape=jax.ShapeDtypeStruct((count_c, plan.padded, LANES), f32),
        compiler_params=pltpu.CompilerParams(
            collective_id=0, has_side_effects=True, vmem_limit_bytes=62 << 20
        ),
        name="far",
    )(
        x, theta_ab, theta_bc, children_b, children_c,
        phi_start_b.reshape(1, -1), phi_weight_b, phi_start_c.reshape(1, -1), phi_weight_c,
        phb, phc, list_src, list_vec, t_view,
    )
    return separate(out, plan.rows)


def solution(mesh):
    placed = (
        P("box", None, "samp"),
        P("box", None),
        P("box", None),
        P(),
        P(),
        P("samp"),
        P(None, "samp"),
        P("samp"),
        P(None, "samp"),
        P(None, None, "samp"),
        P("box", None),
        P("box", None),
    )
    return jax.shard_map(
        functools.partial(per_device, mesh.shape["samp"], mesh.shape["box"]),
        mesh=mesh, in_specs=placed, out_specs=P("box", None, "samp"), check_vma=False,
    )
```

time: 114 us -> 84.5 us (0.74)
  Pallas kernels: 92.4 us -> 79.2 us
  other arithmetic: 9.65 us -> 0 us
  starting transfers between devices: 3.93 us -> 0 us
  local copies, waits for them, and re-layouts: 7.23 us -> 5.09 us
    pallas_call x2 -> x1, Pallas kernels: 92.4 us -> 79.2 us  [per_device(): pl.pallas_call(functools.partial(far_kernel, plan, list_len), in_specs=[h...]
    ppermute x2 -> x0, starting transfers between devices: 3.93 us -> none  [the longest x1 2.97 us: per_device(): lax.ppermute(jnp.concatenate([table_b[:, pb - near:], table_c[:, pc - nea...]
    concatenate x9 -> x0, other arithmetic: 3.93 us -> none  [the longest x1 0.78 us: per_device(): lists = jnp.concatenate([list_src, list_vec], axis=1)]
    dynamic_update_slice x2 -> x0, local copies, waits for them, and re-layouts: 1.72 us -> none  [per_device(): lax.dynamic_update_slice(blocks, theta_ab, (at + k * theta_a, k * theta_b))]
    broadcast_in_dim x2 -> x0, other arithmetic: 1.46 us -> none  [the longest x1 0.81 us: per_device(): phi_start_b.astype(jnp.float32)[None]]
    ge x2 -> x0, other arithmetic: 1.39 us -> none  [one_hot(): children.T.reshape(-1) >= 0]
    transpose x2 -> x0, other arithmetic: 1.38 us -> none  [one_hot(): ids = (children - first).T.reshape(-1)]
    unnamed x6 -> x3, local copies, waits for them, and re-layouts: 4.03 us -> 5.09 us
  transfers between devices with their start and end apart: 2 -> 0, of which waited for: 0 -> 0; matrix products, arithmetic and copies ran while one was open for 8% -> 0% of each run, Pallas kernels for 0% -> 0%
where the time goes in v2:
time: 84.5 us; the launch traced here: 84.3 us
  Pallas kernels  79.2 us (94%)
  local copies, waits for them, and re-layouts  5.09 us (6%)
    pallas_call x1, Pallas kernels, per_device(): pl.pallas_call(functools.partial(far_kernel, plan, list_len), in_specs=[h...  79.2 us
    unnamed x3, local copies, waits for them, and re-layouts  5.09 us

profile of v2, /device:TPU:0, one launch (start us, length us, event | category | flops | bytes accessed | tf_op | source)
XLA Modules:
  0.0 84.3 jit_solution(2586894002542492359)
XLA Ops:
  0.0 1.4 %copy.16.child_b = s32[32,8]{1,0:T(8,128)} copy(s32[32,8]{0,1:T(8,128)} %param.15) | data formatting | bytes 2048 | tf_op args[1]
  1.4 1.6 %copy.15.theta_bc = f32[128,160]{1,0:T(8,128)} copy(f32[128,160]{0,1:T(8,128)} %param.18) | data formatting | bytes 163840 | tf_op args[4]
  3.0 79.2 %far.1 = f32[8,200,128]{2,1,0:T(8,128)} custom-call(f32[128,72,128]{2,1,0:T(8,128)} %bitcast.18, f32[96,128]{1,0:T(8,128)} %theta_ab.1, f32[128,160]{1,0:T(8,128)} %copy.15.theta_bc, s32[32,8]{1,0:T(8,128)} %copy.16.child_b, s32[8,8]{1,0:T(8,128)} %child_c.1, s32[1,64]{1,0:T(1,128)} %bitcast.20, f32[4,64]{1,0:T(4,128)} %weight_b.1, s32[1,80]{1,0:T(1,128)} %bitcast.21, ...), custom_call_target="tpu_custom_call" | custom-call | tf_op jit(solution)/shard_map/far/pallas_call | solution.py:679
  82.2 2.1 %copy.18 = f32[8,2,12800]{2,1,0:T(2,128)} copy(f32[8,2,12800]{2,1,0:T(2,128)} %bitcast.19) | data formatting | bytes 1638400

commit v3 on v2

--- a/solution.py
+++ b/solution.py
@@ -14,7 +14,9 @@
 LANES = 128
 MESH = pl.DeviceIdType.MESH
 GROUP = 4
-FIRST_CHUNKS = (2, 4, 4, 2, 1)
+FIRST_CHUNKS = (2, 4, 3, 3, 1)
+UNROLL_B = 4
+UNROLL_T = 8
 REPS = ((1, 1), (1, -1), (-1, 1), (-1, -1))
 
 
@@ -157,7 +159,7 @@
     plan, list_len,
     x_hbm, theta_ab, theta_bc, child_b, child_c, start_b, weight_b, start_c, weight_c,
     phb_hbm, phc_hbm, src_ref, vec_ref, t_hbm, o_ref,
-    x_ref, grid_a, grid_b, phb, phc, tab, tbc, s_b, s_c, ints, floats, tables_i, tables_w, idx, wgt, wide,
+    x_ref, grid_a, pattern_b, grid_b, phb, phc, tab, tbc, s_b, s_c, ints, floats, tables_i, tables_w, idx, wgt, wide,
     lists, list_all, list_smem, halo_left, halo_right, swapped, res, psend, precv, *rest,
 ):
     n_chunk = len(plan.sizes)
@@ -187,9 +189,9 @@
     for copy in in_copies:
         copy.start()
 
-    count_a, count_b, count_c = x_ref.shape[0], child_b.shape[0], child_c.shape[0]
+    count_a, count_b, count_c = x_ref.shape[0], child_b.shape[1], child_c.shape[0]
     theta_a, theta_b = theta_ab.shape
-    theta_c = theta_bc.shape[1]
+    theta_c = theta_bc.shape[0]
     ints[1, 0:1, 0 : plan.pb] = start_b[...]
     ints[1, 1:2, 0 : plan.pc] = start_c[...]
     floats[1, 0:4, 0 : plan.pb] = weight_b[...]
@@ -219,15 +221,14 @@
             cols = slice(k * theta_b, (k + 1) * theta_b)
             tab[pair, 0, rows, cols] = high
             tab[pair, 1, rows, cols] = low
-    high, low = split(theta_bc[...])
+    high, low = split(theta_bc[...].T)
     tbc[0, :theta_b] = high
     tbc[0, theta_b:] = high
     tbc[1, :theta_b] = low
     tbc[1, theta_b:] = low
     turns = samp // n_base
 
-    def one_hot(child, first, count):
-        ids = child[...]
+    def one_hot(ids, first, count):
         lane = lax.broadcasted_iota(jnp.int32, (ids.shape[0], count), 1) + first
         plus, minus = [], []
         for rep in range(4):
@@ -245,8 +246,8 @@
         hot = jnp.concatenate(plus + minus, axis=0).astype(jnp.bfloat16)
         return jnp.concatenate([hot, hot], axis=1)
 
-    s_b[...] = one_hot(child_b, box * count_a, count_a)
-    s_c[...] = one_hot(child_c, box * count_b, count_b)
+    s_b[...] = one_hot(child_b[...].T, box * count_a, count_a)
+    s_c[...] = one_hot(child_c[...], box * count_b, count_b)
     wide[...] = jnp.zeros(wide.shape, jnp.float32)
     pl.semaphore_wait(barrier, n_box + 1)
 
@@ -371,8 +372,7 @@
             phb[m], picked[:mid, :LANES], picked[:mid, LANES:], picked[mid:, :LANES], picked[mid:, LANES:], count_b
         )
         high, low = split(jnp.concatenate([real, imag], axis=0))
-        both = jnp.concatenate([high, low], axis=1)
-        return mm(both, tbc[0]) + mm(high, tbc[1, :LANES])
+        return jnp.concatenate([high, low], axis=1)
 
     def level_c(g):
         reals, imags = [], []
@@ -433,14 +433,26 @@
         lax.fori_loop(0, count, one_a, 0)
         count_m, item_m = items(1)
 
-        def two_b(i, carry):
-            m0, m1 = item_m(2 * i), item_m(jnp.minimum(2 * i + 1, count_m - 1))
-            v0, v1 = level_b(m0), level_b(m1)
-            grid_b[m0] = v0
-            grid_b[m1] = v1
+        def some_m(i, n):
+            return [item_m(jnp.minimum(n * i + k, count_m - 1)) for k in range(n)]
+
+        def one_b(i, carry):
+            at = some_m(i, UNROLL_B)
+            values = [level_b(m) for m in at]
+            for m, value in zip(at, values):
+                pattern_b[m] = value
             return carry
 
-        lax.fori_loop(0, pick(ph, [-(-n // 2) for n in plan.levels[1][3]]), two_b, 0)
+        def one_theta(i, carry):
+            at = some_m(i, UNROLL_T)
+            both = jnp.concatenate([pattern_b[m] for m in at], axis=0)
+            grid = mm(both, tbc[0]) + mm(both[:, :LANES], tbc[1, :LANES])
+            for k, m in enumerate(at):
+                grid_b[m] = grid[2 * count_b * k : 2 * count_b * (k + 1)]
+            return carry
+
+        lax.fori_loop(0, pick(ph, [-(-n // UNROLL_B) for n in plan.levels[1][3]]), one_b, 0)
+        lax.fori_loop(0, pick(ph, [-(-n // UNROLL_T) for n in plan.levels[1][3]]), one_theta, 0)
         count_g, item_g = items(2)
 
         def one_c(i, carry):
@@ -683,6 +695,7 @@
         scratch_shapes=[
             pltpu.VMEM(x.shape, f32),
             pltpu.VMEM((pa, 2 * count_a, LANES), f32),
+            pltpu.VMEM((plan.wb, 2 * count_b, 2 * theta_b), bf16),
             pltpu.VMEM((plan.wb, 2 * count_b, theta_c), f32),
             pltpu.VMEM(phb.shape[1:], f32),
             pltpu.VMEM(phc.shape[1:], f32),
@@ -727,7 +740,7 @@
         ),
         name="far",
     )(
-        x, theta_ab, theta_bc, children_b, children_c,
+        x, theta_ab, theta_bc.T, children_b.T, children_c,
         phi_start_b.reshape(1, -1), phi_weight_b, phi_start_c.reshape(1, -1), phi_weight_c,
         phb, phc, list_src, list_vec, t_view,
     )

time: 84.5 us -> 66.1 us (0.78)
  Pallas kernels: 79.2 us -> 63.6 us
  local copies, waits for them, and re-layouts: 5.09 us -> 2.09 us
    pallas_call x1, Pallas kernels: 79.2 us -> 63.6 us  [per_device(): pl.pallas_call(functools.partial(far_kernel, plan, list_len), in_specs=[h...]
    unnamed x3 -> x1, local copies, waits for them, and re-layouts: 5.09 us -> 2.09 us
where the time goes in v3:
time: 66.1 us; the launch traced here: 65.7 us
  Pallas kernels  63.6 us (96%)
  local copies, waits for them, and re-layouts  2.09 us (3%)
    pallas_call x1, Pallas kernels, per_device(): pl.pallas_call(functools.partial(far_kernel, plan, list_len), in_specs=[h...  63.6 us
    unnamed x1, local copies, waits for them, and re-layouts  2.09 us

profile of v3, /device:TPU:0, one launch (start us, length us, event | category | flops | bytes accessed | tf_op | source)
XLA Modules:
  0.0 65.7 jit_solution(15203949976684107723)
XLA Ops:
  0.0 63.6 %far.1 = f32[8,200,128]{2,1,0:T(8,128)} custom-call(f32[128,72,128]{2,1,0:T(8,128)} %bitcast.20, f32[96,128]{1,0:T(8,128)} %theta_ab.1, f32[160,128]{1,0:T(8,128)} %bitcast.22, s32[8,32]{1,0:T(8,128)} %bitcast.23, s32[8,8]{1,0:T(8,128)} %child_c.1, s32[1,64]{1,0:T(1,128)} %bitcast.24, f32[4,64]{1,0:T(4,128)} %weight_b.1, s32[1,80]{1,0:T(1,128)} %bitcast.25, ...), custom_call_target="tpu_custom_call" | custom-call | tf_op jit(solution)/shard_map/far/pallas_call | solution.py:691
  63.6 2.1 %copy.16 = f32[8,2,12800]{2,1,0:T(2,128)} copy(f32[8,2,12800]{2,1,0:T(2,128)} %bitcast.21) | data formatting | bytes 1638400

commit v4 on v3

v4 whole, which is shorter than its diff:
```python
import functools

import jax
import jax.numpy as jnp
import numpy as np
from jax import lax
from jax.experimental import pallas as pl
from jax.experimental.layout import Layout, with_layout_constraint
from jax.experimental.pallas import tpu as pltpu
from jax.sharding import PartitionSpec as P

SIZE_B = 8
SIZE_C = 16
LANES = 128
MESH = pl.DeviceIdType.MESH
GROUP = 4
CHUNKS = ((1, 2), (3,), (3,), (2,), (1,), (1,))
UNROLL_B = 6
UNROLL_T = 6
REPS = ((1, 1), (1, -1), (-1, 1), (-1, -1))


def window(first, last, n_child, n_parent):
    low = 0
    while (low - 1) * n_child // n_parent + 2 >= first:
        low -= 1
    high = 0
    while (high + 1) * n_child // n_parent - 2 <= last:
        high += 1
    return low, high + 1


def quarters(parts):
    return parts // 4 if parts % 4 == 0 else parts


def phase_table(parts, per_part, low, high, n_theta, size):
    n_phi = parts * per_part
    theta = np.pi * (np.arange(n_theta) + 0.5) / n_theta
    first = np.arange(quarters(parts))[:, None] * per_part
    phi = 2.0 * np.pi * (first + np.arange(low, high)[None]) / n_phi
    u_x = np.cos(phi)[..., None] * np.sin(theta)
    u_y = np.sin(phi)[..., None] * np.sin(theta)
    u_z = np.broadcast_to(np.cos(theta), u_x.shape)
    psi = np.stack([0.5 * np.pi * size * (s_x * u_x + s_y * u_y + u_z) for s_x, s_y in REPS], axis=2)
    return np.concatenate([np.cos(psi), np.sin(psi)], axis=2).astype(np.float32)


def octant(rep, turns):
    s_x, s_y = REPS[rep]
    for _ in range(turns):
        s_x, s_y = -s_y, s_x
    return 2 * (s_x + 1) + (s_y + 1) + 1


def split(x):
    high = x.astype(jnp.bfloat16)
    return high, (x - high.astype(jnp.float32)).astype(jnp.bfloat16)


def mm(a, b):
    return jnp.dot(a, b, preferred_element_type=jnp.float32)


def pick(index, values):
    if isinstance(index, int):
        return values[index]
    out = jnp.int32(values[0])
    for k in range(1, len(values)):
        out = jnp.where(index == k, values[k], out)
    return out


class Plan:
    def __init__(self, n_samp, n_box, pa, pb, pc, theta_c):
        self.n_samp, self.n_box = n_samp, n_box
        self.pa, self.pb, self.pc = pa, pb, pc
        n_a, n_b, n_c = n_samp * pa, n_samp * pb, n_samp * pc
        self.low_b, self.high_b = window(0, pa - 1, n_a, n_b)
        low_c, high_c = window(self.low_b, self.high_b - 1, n_b, n_c)
        self.ext = -(-max(-low_c, high_c - pc) // GROUP) * GROUP
        self.low_c, self.high_c = -self.ext, pc + self.ext
        self.wb, self.wc = self.high_b - self.low_b, self.high_c - self.low_c
        self.unit_rows = 2 * GROUP * theta_c // LANES
        self.edge, self.inner = self.ext // GROUP, pc // GROUP
        self.rows = rows = self.inner * self.unit_rows
        ext_rows = self.edge * self.unit_rows
        self.padded = -(-rows // 8) * 8
        groups = self.padded // 8
        self.split = -(-groups // 2)
        other = groups - self.split
        self.end_at = (rows - ext_rows) // 8 * 8
        self.left_rows = self.padded - self.end_at
        self.left_pad = rows - ext_rows - self.end_at
        self.right_rows = -(-ext_rows // 8) * 8
        self.left_at = pl.ds(self.padded, self.left_rows)
        self.right_at = pl.ds(self.padded + self.left_rows, self.right_rows)
        self.total = self.padded + self.left_rows + self.right_rows
        touched = max(self.left_rows, self.right_rows) // 8
        self.sizes, self.blocks = [], []
        for block in CHUNKS + ((1,),) * self.split:
            members = []
            for size in block:
                left = other - sum(self.sizes) - (0 if self.blocks else touched)
                if sum(self.sizes) < self.split and (left > 0 or self.blocks and not members):
                    members.append(len(self.sizes))
                    self.sizes.append(min(size, left) if left > 0 else 1)
            if members:
                self.blocks.append(members)
        self.starts = [sum(self.sizes[:c]) for c in range(len(self.sizes))]
        ends = [a + n for a, n in zip(self.starts, self.sizes)]
        self.both = [end <= other for end in ends]
        self.block_of = [k for k, members in enumerate(self.blocks) for _ in members]
        self.block_starts = [self.starts[members[0]] for members in self.blocks]
        self.block_sizes = [sum(self.sizes[c] for c in members) for members in self.blocks]
        self.block_both = [self.both[members[0]] for members in self.blocks]
        self.local = [pl.ds(8 * a, 8 * n) for a, n in zip(self.block_starts, self.block_sizes)]
        self.early = sum(end <= other - touched for end in ends)
        c_low, c_high, b_low, b_high, a_low, a_high = [], [], [], [], [], []
        for c in range(self.early + 1):
            first, last = 0, self.edge * 2 + self.inner
            if c < self.early:
                first = self.edge + 8 * (self.split - ends[c]) // self.unit_rows
                last = min(last, self.edge - (-8 * (self.split + ends[c]) // self.unit_rows))
            c_low.append(first)
            c_high.append(last)
            b0, b1 = 0, self.wb
            if c < self.early:
                b0 = (self.low_c + GROUP * first) * n_b // n_c - 2 - self.low_b
                b1 = (self.low_c + GROUP * last - 1) * n_b // n_c + 3 - self.low_b
                b0, b1 = max(b0, 0), min(b1, self.wb)
                if c:
                    b0, b1 = min(b0, b_low[-1]), max(b1, b_high[-1])
                inside_low, inside_high = -self.low_b, pb - self.low_b
                more = -(b1 - b0 - (b_high[-1] - b_low[-1] if c else 0)) % UNROLL_B
                for k in range(more):
                    if (k % 2 == 0 or b1 >= inside_high) and b0 > inside_low:
                        b0 -= 1
                    elif b1 < inside_high:
                        b1 += 1
            b_low.append(b0)
            b_high.append(b1)
            a0 = max((b0 + self.low_b) * n_a // n_b - 2, 0)
            a1 = min((b1 - 1 + self.low_b) * n_a // n_b + 3, pa)
            if c == self.early:
                a0, a1 = 0, pa
            a_low.append(a0 // GROUP)
            a_high.append(-(-a1 // GROUP))
        inside = [
            b0 + self.low_b >= 0 and b1 + self.low_b <= pb and self.edge <= c0 and c1 <= self.edge + self.inner
            for b0, b1, c0, c1 in zip(b_low, b_high, c_low, c_high)
        ]
        assert all(inside[: self.early]) and self.early
        assert self.early >= len(self.blocks[0]) and self.both[0]
        self.x_low, self.x_high = 6 * a_low[0] // 8 * 8, -(-6 * a_high[0] // 8) * 8
        self.levels = (self.spans(a_low, a_high), self.spans(b_low, b_high), self.spans(c_low, c_high))

    @staticmethod
    def spans(low, high):
        before_low, before_high = [high[0]] + low[:-1], [high[0]] + high[:-1]
        left = [b - a for a, b in zip(low, before_low)]
        count = [n + b - a for n, a, b in zip(left, before_high, high)]
        return low, left, before_high, count


def stencil(plan, samp, start, weight):
    row = lax.broadcasted_iota(jnp.int32, start.shape, 0)
    at_b = row < 4
    n_a, n_b = plan.n_samp * plan.pa, plan.n_samp * plan.pb

    def choose(b, c):
        return jnp.where(at_b, b, c)

    tap = start + choose(row - samp * plan.pa, row - 4 - samp * plan.pb)
    count, half = choose(n_a, n_b), choose(n_a // 2, n_b // 2)
    low, high = choose(0, plan.low_b), choose(plan.pa, plan.high_b)
    centre = choose(plan.pa // 2, (plan.low_b + plan.high_b) // 2)
    for _ in range(2):
        tap = jnp.where(tap - centre > half, tap - count, tap)
        tap = jnp.where(tap - centre < -half, tap + count, tap)
    inside = (tap >= low) & (tap < high)
    return jnp.clip(tap - low, 0, high - low - 1), jnp.where(inside, weight, 0.0)


def far_kernel(plan, list_len, x_hbm, *rest):
    small_hbm, (phb_hbm, phc_hbm, t_hbm, o_ref), small, rest = rest[:10], rest[10:14], rest[14:24], rest[24:]
    (theta_ab, theta_bc, child_b, child_c, start_b, weight_b, start_c, weight_c, src_ref, vec_ref) = small
    (
        x_ref, grid_a, pattern_b, grid_b, phb, phc, tab, tbc,
        s_b, s_c, ints, floats, tables_i, tables_w, idx, wgt,
        wide, lists, list_all, list_smem, halo_left, halo_right, res,
        psend, precv,
        *rest,
    ) = rest
    n_chunk, n_block = len(plan.sizes), len(plan.blocks)
    srcs, tbufs = rest[:n_block], rest[n_block : 2 * n_block]
    (in_sem, table_sem, list_sem, smem_sem, halo_sem, t_sem, src_send, src_recv, p_sem, out_sem) = rest[2 * n_block :]
    samp, box = lax.axis_index("samp"), lax.axis_index("box")
    n_box, n_samp = plan.n_box, plan.n_samp
    n_chip = n_box // 2
    chip, core = box // 2, box % 2
    partner = chip * 2 + 1 - core
    own = wide.shape[0]
    n_src = own * n_box
    first_end, last_end = chip == 0, chip == n_chip - 1
    is_end = first_end | last_end
    helps_first, helps_last = chip == 1, chip == n_chip - 2
    helps = helps_first | helps_last
    helped = jnp.where(helps_first, 0, n_chip - 1)
    helper = jnp.where(first_end, 1, n_chip - 2)
    left = (lax.rem(samp + n_samp - 1, n_samp), box)
    right = (lax.rem(samp + 1, n_samp), box)
    n_base = quarters(n_samp)

    barrier = pltpu.get_barrier_semaphore()
    for other in range(n_box):
        @pl.when(box != other)
        def _():
            pl.semaphore_signal(barrier, inc=1, device_id=(samp, other), device_id_type=MESH)
    for device in (left, right):
        pl.semaphore_signal(barrier, inc=1, device_id=device, device_id_type=MESH)

    x_rows_all = x_hbm.shape[1]
    pieces = [
        (first, last - first)
        for first, last in ((plan.x_low, plan.x_high), (0, plan.x_low), (plan.x_high, x_rows_all))
        if last > first
    ]
    in_copies = []
    for k, (first, n) in enumerate(pieces):
        here = pl.ds(first, n)
        in_copies.append(pltpu.make_async_copy(x_hbm.at[:, here, :], x_ref.at[:, here, :], in_sem.at[k]))
        if k == 0:
            base = lax.rem(samp, n_base)
            in_copies.append(pltpu.make_async_copy(phb_hbm.at[base], phb, in_sem.at[3]))
            in_copies.append(pltpu.make_async_copy(phc_hbm.at[base], phc, in_sem.at[4]))
    small_copies = [
        pltpu.make_async_copy(a, b, in_sem.at[5 + k]) for k, (a, b) in enumerate(zip(small_hbm, small))
    ]
    for copy in small_copies[:1] + in_copies[:1] + small_copies[1:] + in_copies[1:]:
        copy.start()
    small_copies[0].wait()
    count_a, count_b, count_c = x_ref.shape[0], child_b.shape[1], child_c.shape[0]
    theta_a, theta_b = theta_ab.shape
    theta_c = theta_bc.shape[0]
    def remote(src, dst, send, recv, device):
        return pltpu.make_async_remote_copy(
            src_ref=src, dst_ref=dst, send_sem=send, recv_sem=recv, device_id=device, device_id_type=MESH
        )

    tab[...] = jnp.zeros(tab.shape, jnp.bfloat16)
    high, low = split(theta_ab[...])
    for pair in range(2):
        at = pair * (2 * theta_a - LANES)
        for k in range(2):
            rows = slice(at + k * theta_a, at + (k + 1) * theta_a)
            cols = slice(k * theta_b, (k + 1) * theta_b)
            tab[pair, 0, rows, cols] = high
            tab[pair, 1, rows, cols] = low
    turns = samp // n_base

    def one_hot(ids, first, count):
        lane = lax.broadcasted_iota(jnp.int32, (ids.shape[0], count), 1) + first
        plus, minus = [], []
        for rep in range(4):
            hots = []
            for flip in range(2):
                column = None
                for t in range(n_samp // n_base):
                    o = octant(rep, t)
                    o = 7 - o if flip else o
                    here = ids[:, o : o + 1]
                    column = here if column is None else jnp.where(turns == t, here, column)
                hots.append(jnp.where(column == lane, 1.0, 0.0))
            plus.append(hots[0] + hots[1])
            minus.append(hots[0] - hots[1])
        hot = jnp.concatenate(plus + minus, axis=0).astype(jnp.bfloat16)
        return jnp.concatenate([hot, hot], axis=1)

    table_copies = []
    for k, ref in enumerate((ints, floats)):
        for d, (slot, device) in enumerate(((2, left), (0, right))):
            n = 4 * k + 2 * d
            table_copies.append(remote(ref.at[1], ref.at[slot], table_sem.at[n], table_sem.at[n + 1], device))
    def rows_of(which, start, size):
        low, high = 8 * (plan.split - start - size), 8 * (plan.split + start)
        return pl.ds(pl.multiple_of(jnp.where(which == 0, low, high), 8), 8 * size)

    def send_rows(which, c):
        return rows_of(which, plan.starts[c], plan.sizes[c])

    def half_rows(which, k):
        return rows_of(which, plan.block_starts[k], plan.block_sizes[k])

    def inner_rows(which, c):
        k = plan.block_of[c]
        after = plan.starts[c] - plan.block_starts[k]
        before = plan.block_sizes[k] - after - plan.sizes[c]
        return pl.ds(pl.multiple_of(jnp.where(which == 0, 8 * before, 8 * after), 8), 8 * plan.sizes[c])

    def t_copy(c):
        return pltpu.make_async_copy(t_hbm.at[:, half_rows(core, c), :], tbufs[c], t_sem.at[c])

    def when_has(which, c, do):
        if plan.block_both[c]:
            do()
        else:
            pl.when(which == 0)(do)

    to_left = remote(wide.at[:, plan.left_at, :], halo_right, halo_sem.at[0], halo_sem.at[1], left)
    to_right = remote(wide.at[:, plan.right_at, :], halo_left, halo_sem.at[2], halo_sem.at[3], right)

    def list_copy(slot, device, k):
        return remote(lists, list_all.at[slot], list_sem.at[k], list_sem.at[3 + slot], device)

    def src_copy(c, chip_to, d):
        index = c * n_box + chip_to * 2 + d
        return remote(
            wide.at[:, send_rows(d, c), :],
            srcs[plan.block_of[c]].at[pl.ds(pl.multiple_of(own * box, 8), own), inner_rows(d, c), :],
            src_send.at[index],
            src_recv.at[c * n_box + box],
            (samp, chip_to * 2 + d),
        )

    def send_chunk(c, act):
        def to_partner():
            act(src_copy(c, chip, 1 - core))

        when_has(1 - core, plan.block_of[c], to_partner)
        for chip_to in range(1, n_chip - 1):
            @pl.when(chip != chip_to)
            def _():
                for d in range(2):
                    if d == 0 or plan.both[c]:
                        act(src_copy(c, chip_to, d))

    x_rows = x_ref.reshape(count_a * x_ref.shape[1], LANES)
    wide_rows = wide.reshape(own * plan.total, LANES)
    stride_x = x_ref.shape[1]

    def theta_block(q):
        highs, lows = [], []
        for c in range(2):
            tiles = [split(x_rows[pl.ds(6 * q + 2 * j + c, count_a, stride=stride_x), :]) for j in range(3)]
            highs.append([t[0] for t in tiles])
            lows.append([t[1] for t in tiles])
        for pair in range(2):
            here = slice(pair, pair + 2)
            high = jnp.concatenate([jnp.concatenate(h[here], axis=1) for h in highs], axis=0)
            low = jnp.concatenate([jnp.concatenate(h[here], axis=1) for h in lows], axis=0)
            both = mm(high, tab[pair, 0]) + mm(low, tab[pair, 0]) + mm(high, tab[pair, 1])
            for k in range(2):
                grid_a[GROUP * q + 2 * pair + k] = both[:, k * LANES : (k + 1) * LANES]

    def taps(n, per_part, first_row):
        part = jnp.where(n >= 0, 1, 0) + jnp.where(n >= per_part, 1, 0)
        col = n + per_part * (1 - part)
        return [(idx[part, first_row + k, col], wgt[part, first_row + k, col]) for k in range(4)]

    def octants(phase, plus_r, plus_i, minus_r, minus_i, count):
        real = imag = None
        for j in range(4):
            cosine, sine = phase[j : j + 1, :], phase[4 + j : 5 + j, :]
            here = slice(j * count, (j + 1) * count)
            re = plus_r[here] * cosine - minus_i[here] * sine
            im = plus_i[here] * cosine + minus_r[here] * sine
            real, imag = (re, im) if real is None else (real + re, imag + im)
        return real, imag

    def level_b(m):
        stencil_b = taps(m + plan.low_b, plan.pb, 0)
        parts = []
        for c in range(2):
            here = slice(c * count_a, (c + 1) * count_a)
            value = None
            for at, weight in stencil_b:
                term = weight * grid_a[at, here, :]
                value = term if value is None else value + term
            parts.append(split(value))
        stacked = jnp.concatenate(
            [
                jnp.concatenate([parts[0][0], parts[1][0]], axis=1),
                jnp.concatenate([parts[0][1], parts[1][1]], axis=1),
            ],
            axis=0,
        )
        picked = mm(s_b[...], stacked)
        mid = 4 * count_b
        real, imag = octants(
            phb[m], picked[:mid, :LANES], picked[:mid, LANES:], picked[mid:, :LANES], picked[mid:, LANES:], count_b
        )
        high, low = split(jnp.concatenate([real, imag], axis=0))
        return jnp.concatenate([high, low], axis=1)

    def level_c(g):
        values = []
        for i in range(GROUP):
            value = None
            for at, weight in taps(g * GROUP + i + plan.low_c, plan.pc, 4):
                term = weight * grid_b[at]
                value = term if value is None else value + term
            values.append(value)
        high, low = split(jnp.concatenate(values, axis=1))
        rr = mm(s_c[...], jnp.concatenate([high[:count_b], low[:count_b]], axis=0))
        ri = mm(s_c[...], jnp.concatenate([high[count_b:], low[count_b:]], axis=0))
        mid = 4 * count_c
        real, imag = octants(phc[g], rr[:mid], ri[:mid], rr[mid:], ri[mid:], count_c)
        base = jnp.where(
            g < plan.edge,
            plan.padded + plan.left_pad + g * plan.unit_rows,
            jnp.where(
                g < plan.edge + plan.inner,
                (g - plan.edge) * plan.unit_rows,
                plan.padded + plan.left_rows + (g - plan.edge - plan.inner) * plan.unit_rows,
            ),
        )
        for c, flat in enumerate((real, imag)):
            for t in range(plan.unit_rows // 2):
                wide_rows[pl.ds(base + 2 * t + c, own, stride=plan.total), :] = flat[:, t * LANES : (t + 1) * LANES]

    def resolve(parts):
        copies = []
        for part in parts:
            row = lax.broadcasted_iota(jnp.int32, ints.shape[1:], 0)
            start = jnp.where(row < 4, ints[part, 0:1, :], ints[part, 1:2, :])
            at, weight = stencil(plan, samp, start, floats[part])
            tables_i[part] = at
            tables_w[part] = weight
            copies.append(pltpu.make_async_copy(tables_i.at[part], idx.at[part], smem_sem.at[part]))
            copies.append(pltpu.make_async_copy(tables_w.at[part], wgt.at[part], smem_sem.at[3 + part]))
        for copy in copies:
            copy.start()
        return copies

    def rest_of_setup():
        for copy in small_copies[1:]:
            copy.wait()
        ints[1, 0:1, 0 : plan.pb] = start_b[...]
        ints[1, 1:2, 0 : plan.pc] = start_c[...]
        floats[1, 0:4, 0 : plan.pb] = weight_b[...]
        floats[1, 4:8, 0 : plan.pc] = weight_c[...]
        lists[:, 0:list_len] = src_ref[...]
        lists[:, list_len : 2 * list_len] = vec_ref[...]
        own_tables = resolve((1,))
        high, low = split(theta_bc[...].T)
        tbc[0, :theta_b] = high
        tbc[0, theta_b:] = high
        tbc[1, :theta_b] = low
        tbc[1, theta_b:] = low
        s_b[...] = one_hot(child_b[...].T, box * count_a, count_a)
        s_c[...] = one_hot(child_c[...], box * count_b, count_b)
        blank = plan.rows // 8 * 8
        wide[:, blank:, :] = jnp.zeros((own, plan.total - blank, LANES), jnp.float32)
        for copy in own_tables + in_copies[1:3]:
            copy.wait()

    def phase(ph, carry):
        def items(level):
            low, before, after, count = (pick(ph, values) for values in plan.levels[level])
            return count, lambda i: jnp.where(i < before, low + i, after + i - before)

        count, item = items(0)

        def one_a(i, carry):
            theta_block(item(i))
            return carry

        lax.fori_loop(0, count, one_a, 0)
        if isinstance(ph, int):
            for k in range(n_block):
                when_has(core, k, lambda k=k: t_copy(k).start())
            rest_of_setup()
        count_m, item_m = items(1)

        def some_m(i, n):
            return [item_m(jnp.minimum(n * i + k, count_m - 1)) for k in range(n)]

        def one_b(i, carry):
            at = some_m(i, UNROLL_B)
            values = [level_b(m) for m in at]
            for m, value in zip(at, values):
                pattern_b[m] = value
            return carry

        def one_theta(i, carry):
            at = some_m(i, UNROLL_T)
            both = jnp.concatenate([pattern_b[m] for m in at], axis=0)
            grid = mm(both, tbc[0]) + mm(both[:, :LANES], tbc[1, :LANES])
            for k, m in enumerate(at):
                grid_b[m] = grid[2 * count_b * k : 2 * count_b * (k + 1)]
            return carry

        lax.fori_loop(0, pick(ph, [-(-n // UNROLL_B) for n in plan.levels[1][3]]), one_b, 0)
        lax.fori_loop(0, pick(ph, [-(-n // UNROLL_T) for n in plan.levels[1][3]]), one_theta, 0)
        count_g, item_g = items(2)

        def one_c(i, carry):
            level_c(item_g(i))
            return carry

        lax.fori_loop(0, count_g, one_c, 0)
        for c in range(1, 1 if isinstance(ph, int) else plan.early):
            @pl.when(ph == c)
            def _():
                send_chunk(c, lambda copy: copy.start())

        return carry

    even = lax.rem(lax.broadcasted_iota(jnp.int32, (8, LANES), 0), 2) == 0

    def turn(x):
        return jnp.where(even, pltpu.roll(x, 7, 0), pltpu.roll(x, 1, 0))

    def gather_sum(c, slot, i):
        size = plan.block_sizes[c]
        by_same = [jnp.zeros((8, LANES), jnp.float32) for _ in range(size)]
        by_turned = [jnp.zeros((8, LANES), jnp.float32) for _ in range(size)]
        for l in range(list_len):
            s = list_smem[slot, i, l]
            v = list_smem[slot, i, list_len + l]
            for g in range(size):
                here = slice(8 * g, 8 * g + 8)
                t = tbufs[c][v, here, :]
                by_same[g] = by_same[g] + t * srcs[c][s, here, :]
                by_turned[g] = by_turned[g] + t * srcs[c][s, slice(8 * (size + g), 8 * (size + g) + 8), :]
        out = []
        for g in range(size):
            x, y = by_same[g], by_turned[g]
            out.append(jnp.where(even, x - pltpu.roll(x, 7, 0), y + pltpu.roll(y, 1, 0)))
        return out

    def result_copy(c):
        return remote(
            res.at[pl.ds(pl.multiple_of((1 - core) * own, 8), own), plan.local[c], :],
            o_ref.at[:, half_rows(core, c), :],
            out_sem.at[c],
            out_sem.at[n_block + c],
            (samp, partner),
        )

    def result_wait(c):
        return remote(
            res.at[pl.ds(pl.multiple_of((1 - core) * own, 8), own), plan.local[c], :],
            o_ref.at[:, half_rows(1 - core, c), :],
            out_sem.at[c],
            out_sem.at[n_block + c],
            (samp, partner),
        )

    def p_copy(c, chip_to):
        return remote(
            psend.at[:, plan.local[c], :],
            precv.at[:, plan.local[c], :],
            p_sem.at[c],
            p_sem.at[n_block + c],
            (samp, chip_to * 2 + core),
        )

    def prepare(c):
        size = plan.block_sizes[c]
        rows = 8 * size
        srcs[c][pl.ds(pl.multiple_of(own * box, 8), own), 0:rows, :] = wide[:, half_rows(core, c), :]
        srcs[c][n_src] = jnp.zeros((2 * rows, LANES), jnp.float32)
        t_copy(c).wait()

        def arrived(other):
            for send in plan.blocks[c]:
                pltpu.make_async_copy(
                    wide.at[:, send_rows(core, send), :],
                    srcs[c].at[pl.ds(own * other, own), inner_rows(core, send), :],
                    src_recv.at[send * n_box + other],
                ).wait()

        for other in range(n_box):
            here = (box != other) & (jnp.logical_not(is_end) | (chip == other // 2))
            pl.when(here)(functools.partial(arrived, other))

        def swap_some(i, carry):
            for k in range(own):
                for g in range(size):
                    s = own * i + k
                    turned = turn(srcs[c][s, slice(8 * g, 8 * g + 8), :])
                    srcs[c][s, slice(8 * (size + g), 8 * (size + g) + 8), :] = turned
            return carry

        first = jnp.where(is_end, 2 * chip, 0)
        last = jnp.where(is_end, 2 * chip + 2, n_box)
        lax.fori_loop(first, last, swap_some, 0)

    def partial_sums(c):
        place = plan.local[c]

        @pl.when(helps)
        def _():
            def one(p, carry):
                slot, i = 2 + p // own, lax.rem(p, own)
                for g, value in enumerate(gather_sum(c, slot, i)):
                    psend[p, pl.ds(place.start + 8 * g, 8), :] = value
                return carry

            lax.fori_loop(0, 2 * own, one, 0)
            p_copy(c, helped).start()

    def own_sums(c):
        place = plan.local[c]

        def one(p, carry):
            slot, i = p // own, lax.rem(p, own)
            for g, value in enumerate(gather_sum(c, slot, i)):
                res[p, pl.ds(place.start + 8 * g, 8), :] = value
            return carry

        lax.fori_loop(0, 2 * own, one, 0)

    def finish(c):
        own_sums(c)

        @pl.when(jnp.logical_not(is_end))
        def _():
            deliver_plain(c)

    def deliver_plain(c):
        place = plan.local[c]
        o_ref[:, half_rows(core, c), :] = res[pl.ds(pl.multiple_of(core * own, 8), own), place, :]
        result_copy(c).start()

    def deliver_end(c):
        place = plan.local[c]
        p_copy(c, chip).wait_recv()
        res[:, place, :] = res[:, place, :] + precv[:, place, :]
        deliver_plain(c)

    def resolve_lists():
        list_copy(1 - core, (samp, partner), 0).wait_recv()

        @pl.when(helps)
        def _():
            for d in range(2):
                list_copy(2 + d, (samp, partner), 0).wait_recv()

        low = jnp.where(last_end, n_src - 2 * own, 0)
        high = jnp.where(first_end, 2 * own, n_src)
        low_p = jnp.where(helps_first, 2 * own, 0)
        high_p = jnp.where(helps_last, n_src - 2 * own, n_src)
        lane = lax.broadcasted_iota(jnp.int32, list_all.shape[1:], 1)
        for slot in range(4):
            a, b = (low, high) if slot < 2 else (low_p, high_p)
            value = list_all[slot]
            gone = (lane < list_len) & ((value < a) | (value >= b))
            list_all[slot] = jnp.where(gone, n_src, value)
        to_smem = pltpu.make_async_copy(list_all, list_smem, smem_sem.at[6])
        to_smem.start()
        to_smem.wait()

    def later_phase(ph, carry):
        @pl.when(ph == plan.early)
        def _():
            for copy in table_copies:
                copy.wait_recv()
            copies = resolve((0, 2))
            resolve_lists()
            prepare(0)
            partial_sums(0)
            for copy in copies:
                copy.wait()

        return phase(ph, carry)

    in_copies[0].wait()
    phase(0, 0)
    pl.semaphore_wait(barrier, n_box + 1)
    send_chunk(0, lambda copy: copy.start())
    for copy in table_copies:
        copy.start()
    list_copy(core, (samp, partner), 0).start()

    @pl.when(is_end)
    def _():
        for d in range(2):
            list_copy(2 + core, (samp, helper * 2 + d), 1 + d).start()

    list_all[core] = lists[...]
    for copy in in_copies[3:]:
        copy.wait()
    lax.fori_loop(1, plan.early + 1, later_phase, 0)
    to_left.start()
    to_right.start()

    def finish_edges():
        to_left.wait_recv()
        to_right.wait_recv()
        at_end = pl.ds(plan.end_at, halo_right.shape[1])
        wide[:, at_end, :] = wide[:, at_end, :] + halo_right[...]
        at_start = pl.ds(0, halo_left.shape[1])
        wide[:, at_start, :] = wide[:, at_start, :] + halo_left[...]
        for c in range(plan.early, n_chunk):
            send_chunk(c, lambda copy: copy.start())

    finish(0)
    finish_edges()

    def whole_block(k):
        prepare(k)
        partial_sums(k)
        finish(k)

    for k in range(1, n_block):
        when_has(core, k, functools.partial(whole_block, k))

    @pl.when(is_end)
    def _():
        for k in range(n_block):
            when_has(core, k, lambda k=k: deliver_end(k))

    for c in range(n_chunk):
        send_chunk(c, lambda copy: copy.wait_send())
    for k in range(n_block):
        when_has(core, k, lambda k=k: result_copy(k).wait_send())

        @pl.when(helps)
        def _():
            when_has(core, k, lambda: p_copy(k, helped).wait_send())

        when_has(1 - core, k, lambda k=k: result_wait(k).wait_recv())

    for copy in table_copies:
        copy.wait_send()
    to_left.wait_send()
    to_right.wait_send()
    list_copy(core, (samp, partner), 0).wait_send()

    @pl.when(is_end)
    def _():
        for d in range(2):
            list_copy(2 + core, (samp, helper * 2 + d), 1 + d).wait_send()


def interleave(x):
    x = x.reshape(x.shape[0], 2, -1, LANES).transpose(0, 2, 1, 3)
    x = with_layout_constraint(x, Layout(major_to_minor=(0, 1, 2, 3))).reshape(x.shape[0], -1, LANES)
    return jnp.pad(x, ((0, 0), (0, -x.shape[1] % 8), (0, 0))) if x.shape[1] % 8 else x


def separate(x, rows):
    x = x[:, :rows].reshape(x.shape[0], -1, 2, LANES)
    x = with_layout_constraint(x, Layout(major_to_minor=(0, 1, 2, 3)))
    return x.transpose(0, 2, 1, 3).reshape(x.shape[0], 2, -1)


def per_device(
    n_samp, n_box,
    pattern_a, children_b, children_c, theta_ab, theta_bc,
    phi_start_b, phi_weight_b, phi_start_c, phi_weight_c,
    translation, list_src, list_vec,
):
    count_a, count_b, count_c = pattern_a.shape[0], children_b.shape[0], children_c.shape[0]
    theta_a, theta_b = theta_ab.shape
    theta_c = theta_bc.shape[1]
    pa = pattern_a.shape[2] // theta_a
    plan = Plan(n_samp, n_box, pa, phi_start_b.shape[0], phi_start_c.shape[0], theta_c)
    phb = jnp.asarray(phase_table(n_samp, plan.pb, plan.low_b, plan.high_b, theta_b, SIZE_B))
    phc = phase_table(n_samp, plan.pc, plan.low_c, plan.high_c, theta_c, SIZE_C)
    phc = phc.reshape(phc.shape[0], -1, GROUP, 8, theta_c).transpose(0, 1, 3, 2, 4)
    phc = jnp.asarray(phc.reshape(phc.shape[:3] + (-1,)))
    x = interleave(pattern_a)
    t_view = interleave(translation)
    list_len = list_src.shape[1]
    n_src = count_c * n_box
    n_chunk, n_block = len(plan.sizes), len(plan.blocks)
    half = 8 * plan.split
    list_lanes = -(-2 * list_len // LANES) * LANES
    lanes = -(-max(plan.pb, plan.pc) // LANES) * LANES
    vmem = pl.BlockSpec(memory_space=pltpu.VMEM)
    hbm = pl.BlockSpec(memory_space=pl.ANY)
    f32, bf16, i32 = jnp.float32, jnp.bfloat16, jnp.int32
    small = (
        theta_ab, theta_bc.T, children_b.T, children_c,
        phi_start_b.reshape(1, -1), phi_weight_b, phi_start_c.reshape(1, -1), phi_weight_c,
        list_src, list_vec,
    )
    out = pl.pallas_call(
        functools.partial(far_kernel, plan, list_len),
        in_specs=[hbm] * 14,
        out_specs=vmem,
        scratch_shapes=[pltpu.VMEM(a.shape, a.dtype) for a in small]
        + [
            pltpu.VMEM(x.shape, f32),
            pltpu.VMEM((pa, 2 * count_a, LANES), f32),
            pltpu.VMEM((plan.wb, 2 * count_b, 2 * theta_b), bf16),
            pltpu.VMEM((plan.wb, 2 * count_b, theta_c), f32),
            pltpu.VMEM(phb.shape[1:], f32),
            pltpu.VMEM(phc.shape[1:], f32),
            pltpu.VMEM((2, 2, 2 * LANES, 2 * theta_b), bf16),
            pltpu.VMEM((2, 2 * theta_b, theta_c), bf16),
            pltpu.VMEM((8 * count_b, 2 * count_a), bf16),
            pltpu.VMEM((8 * count_c, 2 * count_b), bf16),
            pltpu.VMEM((3, 8, lanes), i32),
            pltpu.VMEM((3, 8, lanes), f32),
            pltpu.VMEM((3, 8, lanes), i32),
            pltpu.VMEM((3, 8, lanes), f32),
            pltpu.SMEM((3, 8, lanes), i32),
            pltpu.SMEM((3, 8, lanes), f32),
            pltpu.VMEM((count_c, plan.total, LANES), f32),
            pltpu.VMEM((count_c, list_lanes), i32),
            pltpu.VMEM((4, count_c, list_lanes), i32),
            pltpu.SMEM((4, count_c, list_lanes), i32),
            pltpu.VMEM((count_c, plan.right_rows, LANES), f32),
            pltpu.VMEM((count_c, plan.left_rows, LANES), f32),
            pltpu.VMEM((2 * count_c, half, LANES), f32),
            pltpu.VMEM((2 * count_c, half, LANES), f32),
            pltpu.VMEM((2 * count_c, half, LANES), f32),
        ]
        + [pltpu.VMEM((n_src + 1, 16 * n, LANES), f32) for n in plan.block_sizes]
        + [pltpu.VMEM((t_view.shape[0], 8 * n, LANES), f32) for n in plan.block_sizes]
        + [
            pltpu.SemaphoreType.DMA((15,)),
            pltpu.SemaphoreType.DMA((8,)),
            pltpu.SemaphoreType.DMA((7,)),
            pltpu.SemaphoreType.DMA((7,)),
            pltpu.SemaphoreType.DMA((4,)),
            pltpu.SemaphoreType.DMA((n_block,)),
            pltpu.SemaphoreType.DMA((n_chunk * n_box,)),
            pltpu.SemaphoreType.DMA((n_chunk * n_box,)),
            pltpu.SemaphoreType.DMA((2 * n_block,)),
            pltpu.SemaphoreType.DMA((2 * n_block,)),
        ],
        out_shape=jax.ShapeDtypeStruct((count_c, plan.padded, LANES), f32),
        compiler_params=pltpu.CompilerParams(
            collective_id=0, has_side_effects=True, vmem_limit_bytes=62 << 20
        ),
        name="far",
    )(x, *small, phb, phc, t_view)
    return separate(out, plan.rows)


def solution(mesh):
    placed = (
        P("box", None, "samp"),
        P("box", None),
        P("box", None),
        P(),
        P(),
        P("samp"),
        P(None, "samp"),
        P("samp"),
        P(None, "samp"),
        P(None, None, "samp"),
        P("box", None),
        P("box", None),
    )
    return jax.shard_map(
        functools.partial(per_device, mesh.shape["samp"], mesh.shape["box"]),
        mesh=mesh, in_specs=placed, out_specs=P("box", None, "samp"), check_vma=False,
    )
```

time: 66.1 us -> 59.6 us (0.902)
  Pallas kernels: 63.6 us -> 57.3 us
    pallas_call x1, Pallas kernels: 63.6 us -> 57.3 us  [per_device(): pl.pallas_call(functools.partial(far_kernel, plan, list_len), in_specs=[h...]
where the time goes in v4:
time: 59.6 us; the launch traced here: 59.4 us
  Pallas kernels  57.3 us (96%)
  local copies, waits for them, and re-layouts  2.09 us (4%)
    pallas_call x1, Pallas kernels, per_device(): pl.pallas_call(functools.partial(far_kernel, plan, list_len), in_specs=[h...  57.3 us
    unnamed x1, local copies, waits for them, and re-layouts  2.09 us

profile of v4, /device:TPU:0, one launch (start us, length us, event | category | flops | bytes accessed | tf_op | source)
XLA Modules:
  0.0 59.4 jit_solution(17740982737054695519)
XLA Ops:
  0.0 57.3 %far.1 = f32[8,200,128]{2,1,0:T(8,128)} custom-call(f32[128,72,128]{2,1,0:T(8,128)} %bitcast.20, f32[96,128]{1,0:T(8,128)} %rest_0_.1, f32[160,128]{1,0:T(8,128)} %bitcast.22, s32[8,32]{1,0:T(8,128)} %bitcast.23, s32[8,8]{1,0:T(8,128)} %rest_3_.1, s32[1,64]{1,0:T(1,128)} %bitcast.24, f32[4,64]{1,0:T(4,128)} %rest_5_.1, s32[1,80]{1,0:T(1,128)} %bitcast.25, ...), custom_call_target="tpu_custom_call" | custom-call | tf_op jit(solution)/shard_map/far/pallas_call | solution.py:782
  57.3 2.1 %copy.16 = f32[8,2,12800]{2,1,0:T(2,128)} copy(f32[8,2,12800]{2,1,0:T(2,128)} %bitcast.21) | data formatting | bytes 1638400

commit v5 on v4

--- a/solution.py
+++ b/solution.py
@@ -152,6 +152,7 @@
         ]
         assert all(inside[: self.early]) and self.early
         assert self.early >= len(self.blocks[0]) and self.both[0]
+        self.edges_late = self.block_both[1] and self.early > self.blocks[1][-1]
         self.x_low, self.x_high = 6 * a_low[0] // 8 * 8, -(-6 * a_high[0] // 8) * 8
         self.levels = (self.spans(a_low, a_high), self.spans(b_low, b_high), self.spans(c_low, c_high))
 
@@ -339,19 +340,23 @@
     wide_rows = wide.reshape(own * plan.total, LANES)
     stride_x = x_ref.shape[1]
 
-    def theta_block(q):
+    def theta_blocks(blocks):
         highs, lows = [], []
-        for c in range(2):
-            tiles = [split(x_rows[pl.ds(6 * q + 2 * j + c, count_a, stride=stride_x), :]) for j in range(3)]
-            highs.append([t[0] for t in tiles])
-            lows.append([t[1] for t in tiles])
+        for q in blocks:
+            for c in range(2):
+                tiles = [split(x_rows[pl.ds(6 * q + 2 * j + c, count_a, stride=stride_x), :]) for j in range(3)]
+                highs.append([t[0] for t in tiles])
+                lows.append([t[1] for t in tiles])
         for pair in range(2):
             here = slice(pair, pair + 2)
             high = jnp.concatenate([jnp.concatenate(h[here], axis=1) for h in highs], axis=0)
             low = jnp.concatenate([jnp.concatenate(h[here], axis=1) for h in lows], axis=0)
             both = mm(high, tab[pair, 0]) + mm(low, tab[pair, 0]) + mm(high, tab[pair, 1])
-            for k in range(2):
-                grid_a[GROUP * q + 2 * pair + k] = both[:, k * LANES : (k + 1) * LANES]
+            for n, q in enumerate(blocks):
+                for k in range(2):
+                    grid_a[GROUP * q + 2 * pair + k] = both[
+                        2 * count_a * n : 2 * count_a * (n + 1), k * LANES : (k + 1) * LANES
+                    ]
 
     def taps(n, per_part, first_row):
         part = jnp.where(n >= 0, 1, 0) + jnp.where(n >= per_part, 1, 0)
@@ -463,10 +468,10 @@
         count, item = items(0)
 
         def one_a(i, carry):
-            theta_block(item(i))
+            theta_blocks([item(2 * i), item(jnp.minimum(2 * i + 1, count - 1))])
             return carry
 
-        lax.fori_loop(0, count, one_a, 0)
+        lax.fori_loop(0, pick(ph, [-(-n // 2) for n in plan.levels[0][3]]), one_a, 0)
         if isinstance(ph, int):
             for k in range(n_block):
                 when_has(core, k, lambda k=k: t_copy(k).start())
@@ -651,7 +656,7 @@
             list_all[slot] = jnp.where(gone, n_src, value)
         to_smem = pltpu.make_async_copy(list_all, list_smem, smem_sem.at[6])
         to_smem.start()
-        to_smem.wait()
+        return to_smem
 
     def later_phase(ph, carry):
         @pl.when(ph == plan.early)
@@ -659,8 +664,9 @@
             for copy in table_copies:
                 copy.wait_recv()
             copies = resolve((0, 2))
-            resolve_lists()
+            to_smem = resolve_lists()
             prepare(0)
+            to_smem.wait()
             partial_sums(0)
             for copy in copies:
                 copy.wait()
@@ -698,32 +704,21 @@
             send_chunk(c, lambda copy: copy.start())
 
     finish(0)
-    finish_edges()
+    if not plan.edges_late:
+        finish_edges()
 
     def whole_block(k):
         prepare(k)
         partial_sums(k)
+        if k == 1 and plan.edges_late:
+            finish_edges()
         finish(k)
 
     for k in range(1, n_block):
         when_has(core, k, functools.partial(whole_block, k))
 
-    @pl.when(is_end)
-    def _():
-        for k in range(n_block):
-            when_has(core, k, lambda k=k: deliver_end(k))
-
     for c in range(n_chunk):
         send_chunk(c, lambda copy: copy.wait_send())
-    for k in range(n_block):
-        when_has(core, k, lambda k=k: result_copy(k).wait_send())
-
-        @pl.when(helps)
-        def _():
-            when_has(core, k, lambda: p_copy(k, helped).wait_send())
-
-        when_has(1 - core, k, lambda k=k: result_wait(k).wait_recv())
-
     for copy in table_copies:
         copy.wait_send()
     to_left.wait_send()
@@ -734,6 +729,20 @@
     def _():
         for d in range(2):
             list_copy(2 + core, (samp, helper * 2 + d), 1 + d).wait_send()
+
+    @pl.when(is_end)
+    def _():
+        for k in range(n_block):
+            when_has(core, k, lambda k=k: deliver_end(k))
+
+    for k in range(n_block):
+        when_has(core, k, lambda k=k: result_copy(k).wait_send())
+
+        @pl.when(helps)
+        def _():
+            when_has(core, k, lambda: p_copy(k, helped).wait_send())
+
+        when_has(1 - core, k, lambda k=k: result_wait(k).wait_recv())
 
 
 def interleave(x):
@@ -825,9 +834,9 @@
             pltpu.SemaphoreType.DMA((2 * n_block,)),
             pltpu.SemaphoreType.DMA((2 * n_block,)),
         ],
-        out_shape=jax.ShapeDtypeStruct((count_c, plan.padded, LANES), f32),
+        out_shape=pltpu.VMEM((count_c, plan.padded, LANES), f32),
         compiler_params=pltpu.CompilerParams(
-            collective_id=0, has_side_effects=True, vmem_limit_bytes=62 << 20
+            collective_id=0, has_side_effects=True, vmem_limit_bytes=56 << 20
         ),
         name="far",
     )(x, *small, phb, phc, t_view)

time: 59.6 us -> 57.7 us (0.968)
  local copies, waits for them, and re-layouts: 2.09 us -> 0.89 us
  Pallas kernels: 57.3 us -> 56.6 us
    unnamed x1, local copies, waits for them, and re-layouts: 2.09 us -> 0.89 us
    pallas_call x1, Pallas kernels: 57.3 us -> 56.6 us  [per_device(): pl.pallas_call(functools.partial(far_kernel, plan, list_len), in_specs=[h...]
where the time goes in v5:
time: 57.7 us; the launch traced here: 57.5 us
  Pallas kernels  56.6 us (98%)
  local copies, waits for them, and re-layouts  0.89 us (2%)
    pallas_call x1, Pallas kernels, per_device(): pl.pallas_call(functools.partial(far_kernel, plan, list_len), in_specs=[h...  56.6 us

profile of v5, /device:TPU:0, one launch (start us, length us, event | category | flops | bytes accessed | tf_op | source)
XLA Modules:
  0.0 57.5 jit_solution(4503869919487211747)
XLA Ops:
  0.0 56.6 %far.1 = f32[8,200,128]{2,1,0:T(8,128)S(1)} custom-call(f32[128,72,128]{2,1,0:T(8,128)} %bitcast.21, f32[96,128]{1,0:T(8,128)} %rest_0_.1, f32[160,128]{1,0:T(8,128)} %bitcast.22, s32[8,32]{1,0:T(8,128)} %bitcast.23, s32[8,8]{1,0:T(8,128)} %rest_3_.1, s32[1,64]{1,0:T(1,128)} %bitcast.24, f32[4,64]{1,0:T(4,128)} %rest_5_.1, s32[1,80]{1,0:T(1,128)} %bitcast.25, ...), custom_call_target="tpu_custom_call" | custom-call | tf_op jit(solution)/shard_map/far/pallas_call | solution.py:791
  56.6 0.9 %copy.16 = f32[8,2,12800]{2,1,0:T(2,128)} copy(f32[8,2,12800]{2,1,0:T(2,128)S(1)} %bitcast.19) | data formatting | bytes 1638400

commit v6 on v5

--- a/solution.py
+++ b/solution.py
@@ -351,7 +351,9 @@
             here = slice(pair, pair + 2)
             high = jnp.concatenate([jnp.concatenate(h[here], axis=1) for h in highs], axis=0)
             low = jnp.concatenate([jnp.concatenate(h[here], axis=1) for h in lows], axis=0)
-            both = mm(high, tab[pair, 0]) + mm(low, tab[pair, 0]) + mm(high, tab[pair, 1])
+            count = high.shape[0]
+            twice = mm(jnp.concatenate([high, low], axis=0), tab[pair, 0])
+            both = twice[:count] + twice[count:] + mm(high, tab[pair, 1])
             for n, q in enumerate(blocks):
                 for k in range(2):
                     grid_a[GROUP * q + 2 * pair + k] = both[

time: 57.7 us -> 57.7 us (level)
  no operation moved by 1% of the time
where the time goes in v6:
time: 57.7 us; the launch traced here: 57.5 us
  Pallas kernels  56.6 us (98%)
  local copies, waits for them, and re-layouts  0.89 us (2%)
    pallas_call x1, Pallas kernels, per_device(): pl.pallas_call(functools.partial(far_kernel, plan, list_len), in_specs=[h...  56.6 us

profile of v6, /device:TPU:0, one launch (start us, length us, event | category | flops | bytes accessed | tf_op | source)
XLA Modules:
  0.0 57.5 jit_solution(18106052376746900771)
XLA Ops:
  0.0 56.6 %far.1 = f32[8,200,128]{2,1,0:T(8,128)S(1)} custom-call(f32[128,72,128]{2,1,0:T(8,128)} %bitcast.21, f32[96,128]{1,0:T(8,128)} %rest_0_.1, f32[160,128]{1,0:T(8,128)} %bitcast.22, s32[8,32]{1,0:T(8,128)} %bitcast.23, s32[8,8]{1,0:T(8,128)} %rest_3_.1, s32[1,64]{1,0:T(1,128)} %bitcast.24, f32[4,64]{1,0:T(4,128)} %rest_5_.1, s32[1,80]{1,0:T(1,128)} %bitcast.25, ...), custom_call_target="tpu_custom_call" | custom-call | tf_op jit(solution)/shard_map/far/pallas_call | solution.py:793
  56.6 0.9 %copy.16 = f32[8,2,12800]{2,1,0:T(2,128)} copy(f32[8,2,12800]{2,1,0:T(2,128)S(1)} %bitcast.19) | data formatting | bytes 1638400
